TPU v7x, 32 devices: a whole 2x2x4 slice. The times are simulated.
32 devices in a mesh: ctx: 8 (over z, x), head: 4 (over y, core).
Axes of the slice: x: 2, y: 2, z: 4, core: 2. Of those that a mesh axis runs over, the one named last changes fastest.
Arguments:
- x_in: bfloat16 [8192, 4096], P('ctx', 'head'), may hold values from -6 to 6
- b_in: bfloat16 [8192, 128], P('ctx'), may hold values from -1.796875 to 1.796875
- c_in: bfloat16 [8192, 128], P('ctx'), may hold values from -1.796875 to 1.796875
- d_out: bfloat16 [8192, 4096], P('ctx', 'head'), may hold values from -0.75 to 0.75
- table: float32 [16, 18], replicated, may hold values from 0 to 3, as said below
- level_index: int32 [8192], P('ctx'), may hold values from 0 to 15
Outputs:
- y_out: bfloat16 [8192, 4096], P('ctx', 'head')
- dx_out: bfloat16 [8192, 4096], P('ctx', 'head')
- d_b: float32 [8192, 128], P(('ctx', 'head'))
- d_c: float32 [8192, 128], P(('ctx', 'head'))
Inputs may be any that keep to these rules, and one draw needn't show every extreme that they name: `table`: entries are positive.
All inputs are finite; a program needn't handle non-finite values.
Results may differ from a plain program's by a relative error of at most 0.006.
Values sent between devices are 32-bit elements; how exact they have to be, the bound alone decides.
A program may use at most 128 MiB of HBM per device.

v0:
```python
import functools

import jax
import jax.numpy as jnp
from jax import lax
from jax.experimental import pallas as pl
from jax.experimental.pallas import tpu as pltpu
from jax.sharding import PartitionSpec as P

F32 = jnp.float32
BF16 = jnp.bfloat16
MESH = pl.DeviceIdType.MESH
TILE = 256
WIDTH = 256
VMEM_BYTES = 67043328
SPARE = 16384


def mm(a, b):
    return jnp.dot(a, b, preferred_element_type=F32)


def mm_tn(a, b):
    return lax.dot_general(a, b, (((0,), (0,)), ((), ())), preferred_element_type=F32)


def mm_nt(a, b):
    return lax.dot_general(a, b, (((1,), (1,)), ((), ())), preferred_element_type=F32)


def bit_count(values, bits):
    counted = jnp.zeros(values.shape, jnp.int32)
    for digit_no in range(bits):
        counted = counted + (values >= 1 << digit_no).astype(jnp.int32)
    return counted


def kernel(
    count,
    heads,
    x_hbm,
    b_hbm,
    c_hbm,
    d_hbm,
    table_hbm,
    index_hbm,
    y_ref,
    dx_ref,
    db_ref,
    dc_ref,
    x_ref,
    d_ref,
    b_ref,
    c_ref,
    table_ref,
    index_ref,
    wide_table,
    w_ref,
    y_acc,
    dx_acc,
    grads,
    rise,
    rise_t,
    carry,
    s_buf,
    g_buf,
    rx0,
    up,
    rc,
    rb,
    tot,
    xb,
    rxb,
    *rest,
):
    bits = count.bit_length() - 1
    head_bits = heads.bit_length() - 1
    r_in = rest[:head_bits]
    r_out = rest[head_bits : 2 * head_bits - 1]
    sems = rest[2 * head_bits - 1 :]
    small_sem, in_sem, x0_s, x0_r, up_s, fw_s, rc_r, bk_s, rb_r, xb_s, xb_r = sems[:11]
    hd_sems = sems[11:]
    toks, feats = x_ref.shape
    nstate = b_ref.shape[1]
    chunks = feats // WIDTH
    blocks = toks // TILE
    tile_bits = TILE.bit_length() - 1
    low_bits = toks.bit_length() - 1
    me = lax.axis_index("ctx")
    head = lax.axis_index("head")
    par = me % 2
    col = me // 2
    levels = range(1, bits)
    columns = count // 2
    is_set = {k: (me // (1 << k)) % 2 == 1 for k in range(bits)}
    low_top = {k: col % (1 << k) == (1 << (k - 1)) - 1 for k in levels}
    up_top = {k: col % (1 << k) == (1 << k) - 1 for k in levels}
    relay = {k: is_set[k] & jnp.logical_not(up_top[k]) for k in levels}
    last = col == columns - 1
    ready = {k: up_top[k] & last for k in levels}
    early = {k: up_top[k] & jnp.logical_not(last) for k in levels}
    late = {k: up_top[k] & last for k in levels}

    def fill(hbm, vmem, n, q):
        cols = pl.ds(q * WIDTH, WIDTH)
        return pltpu.make_async_copy(hbm.at[:, cols], vmem.at[:, cols], in_sem.at[n, q])

    smalls = [
        pltpu.make_async_copy(hbm, vmem, small_sem.at[n])
        for n, (hbm, vmem) in enumerate(
            (
                (b_hbm, b_ref),
                (c_hbm, c_ref),
                (table_hbm, table_ref),
                (index_hbm, index_ref),
            )
        )
    ]
    smalls[0].start()
    for q in range(chunks):
        fill(x_hbm, x_ref, 0, q).start()
    for small in smalls[1:]:
        small.start()
    for q in range(chunks):
        fill(d_hbm, d_ref, 1, q).start()

    partner = me + 1 - 2 * par
    barrier = pltpu.get_barrier_semaphore()
    pl.semaphore_signal(barrier, inc=1, device_id={"ctx": partner}, device_id_type=MESH)
    for digit in range(head_bits):
        flip = 1 - 2 * ((head // (1 << digit)) % 2)
        pl.semaphore_signal(
            barrier, inc=1, device_id={"head": head + flip * (1 << digit)}, device_id_type=MESH
        )

    @pl.when(col > 0)
    def _():
        pl.semaphore_signal(barrier, inc=1, device_id={"ctx": me - 2}, device_id_type=MESH)

    @pl.when(col < columns - 1)
    def _():
        pl.semaphore_signal(barrier, inc=1, device_id={"ctx": me + 2}, device_id_type=MESH)

    def remote(src, dst, ssem, rsem, device):
        return pltpu.make_async_remote_copy(
            src_ref=src,
            dst_ref=dst,
            send_sem=ssem,
            recv_sem=rsem,
            device_id=device,
            device_id_type=MESH,
        )

    def x0_copy(q):
        return remote(s_buf.at[q], rx0.at[q], x0_s.at[q], x0_r.at[q], {"ctx": partner})

    def up_copy(k, q):
        return remote(
            up.at[q], rc.at[k - 1, q], up_s.at[q], rc_r.at[k - 1, q], {"ctx": me + 2}
        )

    def forward_copy(k, q):
        return remote(
            rc.at[k - 1, q],
            rc.at[k - 1, q],
            fw_s.at[k - 1, q],
            rc_r.at[k - 1, q],
            {"ctx": me + 2},
        )

    def back_copy(k, q):
        return remote(
            g_buf.at[k, q],
            rb.at[k - 1, q],
            bk_s.at[k - 1, q],
            rb_r.at[k - 1, q],
            {"ctx": me - 2},
        )

    def xb_copy(q):
        return remote(xb.at[q], rxb.at[q], xb_s.at[q], xb_r.at[q], {"ctx": partner})

    smalls[0].wait()
    b_t = b_ref[...].astype(F32).T.astype(BF16)
    ends = (col > 0).astype(jnp.int32) + (col < columns - 1).astype(jnp.int32)
    pl.semaphore_wait(barrier, 1 + head_bits + ends)

    for q in range(chunks):
        cols = slice(q * WIDTH, (q + 1) * WIDTH)
        fill(x_hbm, x_ref, 0, q).wait()
        s_buf[q] = mm(b_t, x_ref[:, cols])
        x0_copy(q).start()

    for small in smalls[1:]:
        small.wait()
    wide_table[...] = jnp.zeros_like(wide_table)
    wide_table[:, : table_ref.shape[1]] = table_ref[...]
    hot = (
        lax.broadcasted_iota(jnp.int32, (table_ref.shape[0], toks), 0) == index_ref[...]
    ).astype(F32)
    w_t = lax.dot_general(
        wide_table[...],
        hot,
        (((0,), (0,)), ((), ())),
        preferred_element_type=F32,
        precision=lax.Precision.HIGHEST,
    )
    w_ref[...] = w_t.T
    c_f = c_ref[...].astype(F32)
    c_t = c_f.T
    for k in range(bits):
        lam_t = w_t[low_bits + 1 + k : low_bits + 2 + k, :]
        rise_t[k * nstate : (k + 1) * nstate, :] = (c_t * lam_t).astype(BF16)

    for q in range(chunks):
        cols = slice(q * WIDTH, (q + 1) * WIDTH)
        fill(d_hbm, d_ref, 1, q).wait()
        g_buf[:, q] = mm(rise_t[...], d_ref[:, cols]).reshape(bits, nstate, WIDTH)
        if bits > 1:

            @pl.when(ready[bits - 1])
            def _():
                back_copy(bits - 1, q).start()

    for k in reversed(range(1, bits - 1)):
        for q in range(chunks):

            @pl.when(ready[k])
            def _():
                back_copy(k, q).start()

    def tile(i, j):
        rows = slice(i * TILE, (i + 1) * TILE)
        cols = slice(j * TILE, (j + 1) * TILE)
        w_rows = w_ref[rows, :]
        if i == j:
            row = lax.broadcasted_iota(jnp.int32, (TILE, TILE), 0)
            at = lax.broadcasted_iota(jnp.int32, (TILE, TILE), 1)
            level = bit_count(row ^ at, tile_bits)
            weight = jnp.zeros((TILE, TILE), F32)
            for n in range(tile_bits + 1):
                weight = jnp.where(level == n, w_rows[:, n : n + 1], weight)
            weight = jnp.where(at <= row, weight, 0.0)
        else:
            level = tile_bits + (i ^ j).bit_length()
            weight = w_rows[:, level : level + 1]
        x_j, d_i, b_j, c_i = x_ref[cols, :], d_ref[rows, :], b_ref[cols, :], c_ref[rows, :]
        mix = (mm_nt(c_i, b_j) * weight).astype(BF16)
        d_mix = (mm_nt(d_i, x_j) * weight).astype(BF16)
        y_t, dx_t = mm(mix, x_j), mm_tn(mix, d_i)
        dc_t, db_t = mm(d_mix, b_j), mm_tn(d_mix, c_i)
        if i == j:
            y_acc[rows, :] = y_t
            dx_acc[cols, :] = dx_t
            grads[1, rows, :] = dc_t
            grads[0, cols, :] = db_t
        else:
            y_acc[rows, :] += y_t
            dx_acc[cols, :] += dx_t
            grads[1, rows, :] += dc_t
            grads[0, cols, :] += db_t

    def pass_up(q):
        x0_copy(q).wait_recv()
        for k in levels:

            @pl.when(low_top[k])
            def _():
                group = s_buf[q] + rx0[q]
                for j in range(1, k):
                    up_copy(j, q).wait_recv()
                    group = group + rc[j - 1, q]
                up[q] = group
                up_copy(k, q).start()

    def relay_up(q):
        for k in levels:

            @pl.when(relay[k])
            def _():
                up_copy(k, q).wait_recv()
                forward_copy(k, q).start()

    def relay_down(q):
        for k in reversed(levels):

            @pl.when(relay[k])
            def _():
                back_copy(k, q).wait_recv()
                g_buf[k, q] = g_buf[k, q] + rb[k - 1, q]
                back_copy(k, q).start()

    def pass_down(q):
        @pl.when(last)
        def _():
            tot[q] = jnp.zeros_like(tot[q])

        for k in levels:

            @pl.when(low_top[k])
            def _():
                back_copy(k, q).wait_recv()
                got = rb[k - 1, q]
                tot[q] = got
                for j in range(1, k):
                    g_buf[j, q] = g_buf[j, q] + got
                    back_copy(j, q).start()

        @pl.when(par == 1)
        def _():
            xb[q] = tot[q] + g_buf[0, q]

        @pl.when(par == 0)
        def _():
            xb[q] = tot[q]

        xb_copy(q).start()

    def far_up(q):
        cols = slice(q * WIDTH, (q + 1) * WIDTH)
        for k in range(bits):
            at = slice(k * nstate, (k + 1) * nstate)
            if k:

                @pl.when(late[k])
                def _():
                    up_copy(k, q).wait_recv()

            @pl.when(is_set[k])
            def _():
                carry[at, :] = (rc[k - 1, q] if k else rx0[q]).astype(BF16)

            @pl.when(jnp.logical_not(is_set[k]))
            def _():
                carry[at, :] = jnp.zeros((nstate, WIDTH), BF16)

        y_ref[:, cols] = (y_acc[:, cols] + mm(rise[...], carry[...])).astype(BF16)
        for i in range(blocks):
            rows = slice(i * TILE, (i + 1) * TILE)
            terms = mm_nt(d_ref[rows, cols], carry[...])
            total = grads[1, rows, :]
            for k in range(bits):
                lam = w_ref[rows, low_bits + 1 + k : low_bits + 2 + k]
                total = total + terms[:, k * nstate : (k + 1) * nstate] * lam
            grads[1, rows, :] = total

    def far_down(q):
        cols = slice(q * WIDTH, (q + 1) * WIDTH)
        xb_copy(q).wait_recv()
        back = (tot[q] + rxb[q]).astype(BF16)
        dx_ref[:, cols] = (dx_acc[:, cols] + mm(b_ref[...], back)).astype(BF16)
        grads[0] = grads[0] + mm_nt(x_ref[:, cols], back)

    part = toks // heads
    waits = []

    def piece(array, digit, g, which):
        if digit == 0:
            start = pl.multiple_of((2 * g + which) * part, part)
            return grads.at[array, pl.ds(start, part)]
        return r_out[digit - 1].at[array, 2 * g + which]

    def halve_start(array, digit):
        mine = (head // (1 << digit)) % 2
        peer = head + (1 - 2 * mine) * (1 << digit)
        copies = []
        for g in range(heads >> (digit + 1)):
            copies.append(
                remote(
                    piece(array, digit, g, 1 - mine),
                    r_in[digit].at[array, g],
                    hd_sems[2 * digit].at[array, g],
                    hd_sems[2 * digit + 1].at[array, g],
                    {"head": peer},
                )
            )
            copies[-1].start()
        waits.extend(copies)
        return copies

    def halve_end(array, digit, copies):
        mine = (head // (1 << digit)) % 2
        for g, copy in enumerate(copies):
            copy.wait_recv()
            value = piece(array, digit, g, mine)[...] + r_in[digit][array, g]
            if digit < head_bits - 1:
                r_out[digit][array, g] = value
            else:
                (db_ref, dc_ref)[array][...] = value

    tiles = [(i, i) for i in range(blocks)]
    tiles += [(i, j) for i in range(blocks) for j in range(i)]

    def near(amount):
        for _ in range(min(amount, len(tiles))):
            tile(*tiles.pop(0))

    def pass_down_if(condition, q):
        @pl.when(condition)
        def _():
            pass_down(q)

    slow = low_top[1] if bits > 1 else col < 0
    quick = jnp.logical_not(slow)
    slots = chunks + 2
    for n in range(slots):
        if n < chunks:
            pass_up(n)
        if 0 < n <= chunks:
            relay_down(n - 1)
        if n > 1:
            pass_down_if(quick, n - 2)
        near(pl.cdiv(len(tiles), slots - n))
    for k in range(bits):
        lam = w_ref[:, low_bits + 1 + k : low_bits + 2 + k]
        rise[:, k * nstate : (k + 1) * nstate] = (c_f * lam).astype(BF16)
    for n in range(chunks + 1):
        if n < chunks:
            relay_up(n)
        if n:
            pass_down_if(slow, n - 1)
        if n < chunks:
            far_up(n)
    jobs = halve_start(1, 0) if head_bits else []
    for n in range(chunks):
        far_down(n)
        if n == max(chunks // 2 - 1, 0) and head_bits:
            halve_end(1, 0, jobs)
            jobs = halve_start(1, 1) if head_bits > 1 else []
    for digit in range(head_bits):
        jobs_b = halve_start(0, digit)
        if digit:
            halve_end(1, digit, jobs)
            jobs = halve_start(1, digit + 1) if digit < head_bits - 1 else []
        halve_end(0, digit, jobs_b)
    if not head_bits:
        db_ref[...] = grads[0]
        dc_ref[...] = grads[1]

    for copy in waits:
        copy.wait_send()
    for q in range(chunks):
        x0_copy(q).wait_send()
        xb_copy(q).wait_send()
        for k in levels:

            @pl.when(low_top[k])
            def _():
                up_copy(k, q).wait_send()

            @pl.when(relay[k])
            def _():
                forward_copy(k, q).wait_send()

            @pl.when(is_set[k])
            def _():
                back_copy(k, q).wait_send()


def write_out(*refs):
    copies = [pltpu.make_async_copy(refs[n], refs[n + 4], refs[8].at[n]) for n in range(4)]
    for copy in copies:
        copy.start()
    for copy in copies:
        copy.wait()


def local(x_in, b_in, c_in, d_out, table, level_index):
    toks, feats = x_in.shape
    nstate = b_in.shape[1]
    count, heads = lax.axis_size("ctx"), lax.axis_size("head")
    bits, head_bits = count.bit_length() - 1, heads.bit_length() - 1
    chunks = feats // WIDTH
    index = level_index.reshape(1, toks)
    rows = toks // heads
    ups = max(bits - 1, 1)
    vmem = pl.BlockSpec(memory_space=pltpu.VMEM)
    hbm = pl.BlockSpec(memory_space=pltpu.HBM)
    dma = pltpu.SemaphoreType.DMA
    slab = (chunks, nstate, WIDTH)
    halves = [heads >> (n + 1) for n in range(head_bits)]
    results = pl.pallas_call(
        functools.partial(kernel, count, heads),
        out_shape=(
            pltpu.VMEM((toks, feats), BF16),
            pltpu.VMEM((toks, feats), BF16),
            pltpu.VMEM((rows, nstate), F32),
            pltpu.VMEM((rows, nstate), F32),
        ),
        in_specs=[hbm] * 6,
        out_specs=(vmem,) * 4,
        scratch_shapes=[
            pltpu.VMEM((toks, feats), BF16),
            pltpu.VMEM((toks, feats), BF16),
            pltpu.VMEM((toks, nstate), BF16),
            pltpu.VMEM((toks, nstate), BF16),
            pltpu.VMEM(table.shape, F32),
            pltpu.VMEM((1, toks), jnp.int32),
            pltpu.VMEM((table.shape[0], nstate), F32),
            pltpu.VMEM((toks, nstate), F32),
            pltpu.VMEM((toks, feats), F32),
            pltpu.VMEM((toks, feats), F32),
            pltpu.VMEM((2, toks, nstate), F32),
            pltpu.VMEM((toks, bits * nstate), BF16),
            pltpu.VMEM((bits * nstate, toks), BF16),
            pltpu.VMEM((bits * nstate, WIDTH), BF16),
            pltpu.VMEM(slab, F32),
            pltpu.VMEM((bits,) + slab, F32),
            pltpu.VMEM(slab, F32),
            pltpu.VMEM(slab, F32),
            pltpu.VMEM((ups,) + slab, F32),
            pltpu.VMEM((ups,) + slab, F32),
            pltpu.VMEM(slab, F32),
            pltpu.VMEM(slab, F32),
            pltpu.VMEM(slab, F32),
        ]
        + [pltpu.VMEM((2, half, rows, nstate), F32) for half in halves]
        + [pltpu.VMEM((2, half, rows, nstate), F32) for half in halves[:-1]]
        + [
            dma((4,)),
            dma((2, chunks)),
            dma((chunks,)),
            dma((chunks,)),
            dma((chunks,)),
            dma((ups, chunks)),
            dma((ups, chunks)),
            dma((ups, chunks)),
            dma((ups, chunks)),
            dma((chunks,)),
            dma((chunks,)),
        ]
        + [dma((2, half)) for half in halves for _ in range(2)],
        compiler_params=pltpu.CompilerParams(
            collective_id=0, has_side_effects=True, vmem_limit_bytes=VMEM_BYTES - 4 * toks * feats - 8 * rows * nstate - SPARE
        ),
    )(x_in, b_in, c_in, d_out, table, index)
    return pl.pallas_call(
        write_out,
        out_shape=tuple(jax.ShapeDtypeStruct(r.shape, r.dtype) for r in results),
        in_specs=[vmem] * 4,
        out_specs=(hbm,) * 4,
        scratch_shapes=[dma((4,))],
        compiler_params=pltpu.CompilerParams(vmem_limit_bytes=1024 * 1024),
    )(*results)


def solution(mesh):
    return jax.shard_map(
        local,
        mesh=mesh,
        in_specs=(
            P("ctx", "head"),
            P("ctx", None),
            P("ctx", None),
            P("ctx", "head"),
            P(),
            P("ctx"),
        ),
        out_specs=(
            P("ctx", "head"),
            P("ctx", "head"),
            P(("ctx", "head"), None),
            P(("ctx", "head"), None),
        ),
        check_vma=False,
    )
```

profile of v0, /device:TPU:0, one launch (start us, length us, event | category | flops | bytes accessed | tf_op | source)
XLA Modules:
  0.0 46.1 jit_solution(1360510522022385426)
XLA Ops:
  0.6 43.1 %shard_map.93 = (bf16[1024,1024]{1,0:T(8,128)(2,1)S(1)}, bf16[1024,1024]{1,0:T(8,128)(2,1)S(1)}, f32[256,128]{1,0:T(8,128)S(1)}, f32[256,128]{1,0:T(8,128)S(1)}) custom-call(bf16[1024,1024]{1,0:T(8,128)(2,1)} %x_hbm.1, bf16[1024,128]{1,0:T(8,128)(2,1)} %b_hbm.1, bf16[1024,128]{1,0:T(8,128)(2,1)} %c_hbm.1, bf16[1024,1024]{1,0:T(8,128)(2,1)} %d_hbm.1, ...), custom_call_target="tpu_custom_call" | custom-call | tf_op jit(solution)/shard_map/pallas_call | solution.py:482
  43.8 2.1 %shard_map.94 = (bf16[1024,1024]{1,0:T(8,128)(2,1)}, bf16[1024,1024]{1,0:T(8,128)(2,1)}, f32[256,128]{1,0:T(8,128)}, f32[256,128]{1,0:T(8,128)}) custom-call(bf16[1024,1024]{1,0:T(8,128)(2,1)S(1)} %get-tuple-element.8.refs_0_, bf16[1024,1024]{1,0:T(8,128)(2,1)S(1)} %get-tuple-element.9.refs_1_, f32[256,128]{1,0:T(8,128)S(1)} %get-tuple-element.10.refs_2_, ...), custom_call_target="tpu_custom_call" | custom-call | tf_op jit(solution)/shard_map/pallas_call | solution.py:537
where the time goes:
time: 46.3 us; the launch traced here: 46.1 us
  Pallas kernels  45.2 us (98%)
  between operations  0.8 us (2%)
    pallas_call x1, Pallas kernels, local(): pl.pallas_call(functools.partial(kernel, count, heads), out_shape=(pltpu....  43.1 us
    pallas_call x1, Pallas kernels, local(): pl.pallas_call(write_out, out_shape=tuple((jax.ShapeDtypeStruct(r.shape,...  2.11 us

commit v1 on v0

v1 whole, which is shorter than its diff:
```python
import contextlib
import functools

import jax
import jax.numpy as jnp
from jax import lax
from jax.experimental import pallas as pl
from jax.experimental.pallas import tpu as pltpu
from jax.sharding import PartitionSpec as P

F32 = jnp.float32
BF16 = jnp.bfloat16
MESH = pl.DeviceIdType.MESH
TILE = 256
WIDTH = 256
CHUNKS = 16
GROUPS = ((0, 8), (8, 14), (14, 16))
FAR_AT = ((21.5, 22.9), (25.3, 26.6), (26.8, 28.0))
EARLY = 2
BEAT = 0.7
UP_SPLIT = range(1, 15)
DOWN_SPLIT = range(1, 11)
TOP_SPLIT = range(12, 16)
VMEM_BYTES = 67043328
SPARE = 16384


def scope(name):
    return contextlib.nullcontext()


def mm(a, b):
    return jnp.dot(a, b, preferred_element_type=F32)


def mm_tn(a, b):
    return lax.dot_general(a, b, (((0,), (0,)), ((), ())), preferred_element_type=F32)


def mm_nt(a, b):
    return lax.dot_general(a, b, (((1,), (1,)), ((), ())), preferred_element_type=F32)


def bit_count(values, bits):
    counted = jnp.zeros(values.shape, jnp.int32)
    for digit_no in range(bits):
        counted = counted + (values >= 1 << digit_no).astype(jnp.int32)
    return counted


def kernel(
    count,
    heads,
    x_hbm,
    b_hbm,
    c_hbm,
    d_hbm,
    table_hbm,
    index_hbm,
    y_ref,
    dx_ref,
    db_ref,
    dc_ref,
    x_ref,
    d_ref,
    b_ref,
    c_ref,
    table_ref,
    index_ref,
    wide_table,
    w_ref,
    wt_ref,
    bt_ref,
    ct_ref,
    mix,
    d_mix,
    y_acc,
    dx_acc,
    grads,
    rise,
    rise_t,
    carry,
    back,
    s_buf,
    g_buf,
    rx0,
    up,
    rc,
    rb,
    tot,
    xb,
    rxb,
    hr,
    small_sem,
    x_sem,
    d_sem,
    x0_s,
    x0_r,
    up_s,
    fw_s,
    rc_r,
    ga_s,
    pr_s,
    bk_s,
    rb_r,
    xb_s,
    xb_r,
    hd_s,
    hd_r,
):
    bits = count.bit_length() - 1
    top = bits - 1
    toks, feats = x_ref.shape
    nstate = b_ref.shape[1]
    rows_q = nstate // CHUNKS
    blocks = toks // TILE
    part = toks // heads
    tile_bits = TILE.bit_length() - 1
    low_bits = toks.bit_length() - 1
    me = lax.axis_index("ctx")
    head = lax.axis_index("head")
    par = me % 2
    col = me // 2
    levels = range(1, bits)
    columns = count // 2
    split = bits >= 3
    is_set = {k: (me // (1 << k)) % 2 == 1 for k in range(bits)}
    low_top = {k: col % (1 << k) == (1 << (k - 1)) - 1 for k in levels}
    up_top = {k: col % (1 << k) == (1 << k) - 1 for k in levels}
    relay = {k: is_set[k] & jnp.logical_not(up_top[k]) for k in levels}
    last = col == columns - 1
    inner = jnp.logical_not(last)
    beside = col == columns - 2
    mine = (par == 0, par == 1)
    partner = me + 1 - 2 * par

    def splits_up(k, q):
        return split and k < top and q in UP_SPLIT

    def splits_down(k, q):
        return split and q in (DOWN_SPLIT if k < top else TOP_SPLIT)

    def owned(splits, k, line):
        return sum(not splits(k, q) or q % 2 == line for q in range(CHUNKS))

    def shared(splits, k, line):
        return sum(splits(k, q) and q % 2 == line for q in range(CHUNKS))

    def carried_up(k, q):
        return jnp.logical_not(beside) | mine[q % 2] if splits_up(k, q) else None

    def carried_down(k, q):
        return jnp.logical_not(beside) | mine[q % 2] if splits_down(k, q) else None

    def when(condition, body):
        if condition is None:
            body()
        else:
            pl.when(condition)(body)

    strips = feats // WIDTH
    loads = [
        pltpu.make_async_copy(hbm, vmem, small_sem.at[n])
        for n, (hbm, vmem) in enumerate(
            (
                (table_hbm, table_ref),
                (index_hbm, index_ref),
                (c_hbm, c_ref),
                (b_hbm, b_ref),
            )
        )
    ]
    halves = 2
    wide = feats // halves

    def fill_x(n):
        cols = pl.ds(n * wide, wide)
        return pltpu.make_async_copy(x_hbm.at[:, cols], x_ref.at[:, cols], x_sem.at[n])

    fill_d = pltpu.make_async_copy(d_hbm, d_ref, d_sem.at[0])
    for load in loads:
        load.start()
    for n in range(halves):
        fill_x(n).start()

    barrier = pltpu.get_barrier_semaphore()
    pl.semaphore_signal(barrier, inc=1, device_id={"ctx": partner}, device_id_type=MESH)

    @pl.when(col > 0)
    def _():
        pl.semaphore_signal(barrier, inc=1, device_id={"ctx": me - 2}, device_id_type=MESH)

    @pl.when(inner)
    def _():
        pl.semaphore_signal(barrier, inc=1, device_id={"ctx": me + 2}, device_id_type=MESH)

    peers = [(head + m) % heads for m in range(1, heads)]
    for peer in peers:
        pl.semaphore_signal(barrier, inc=1, device_id={"head": peer}, device_id_type=MESH)

    def remote(src, dst, ssem, rsem, device):
        return pltpu.make_async_remote_copy(
            src_ref=src,
            dst_ref=dst,
            send_sem=ssem,
            recv_sem=rsem,
            device_id=device,
            device_id_type=MESH,
        )

    def x0_copy(q):
        return remote(s_buf.at[q], rx0.at[q], x0_s.at[0], x0_r.at[q], {"ctx": partner})

    def up_copy(k, q):
        return remote(up.at[q], rc.at[k - 1, q], up_s.at[0], rc_r.at[k - 1, q], {"ctx": me + 2})

    def forward_copy(k, q):
        held = rc.at[k - 1, q]
        return remote(held, held, fw_s.at[k - 1], rc_r.at[k - 1, q], {"ctx": me + 2})

    def gather_copy(k, q):
        held = rc.at[k - 1, q]
        return remote(held, held, ga_s.at[k - 1], rc_r.at[k - 1, q], {"ctx": partner})

    def pre_copy(k, q):
        return remote(
            g_buf.at[k, q], rb.at[k - 1, q], pr_s.at[k - 1], rb_r.at[k - 1, q], {"ctx": partner}
        )

    def back_copy(k, q):
        return remote(
            g_buf.at[k, q], rb.at[k - 1, q], bk_s.at[k - 1], rb_r.at[k - 1, q], {"ctx": me - 2}
        )

    def group_of(q):
        return next(g for g, (q0, q1) in enumerate(GROUPS) if q0 <= q < q1)

    def xb_copy(q):
        return remote(xb.at[q], rxb.at[q], xb_s.at[0], xb_r.at[group_of(q)], {"ctx": partner})

    def xg_copy(q):
        return remote(
            g_buf.at[0, q], rxb.at[q], xb_s.at[0], xb_r.at[group_of(q)], {"ctx": partner}
        )

    def xb_all(q0, n, g):
        held = pl.ds(q0, n)
        return remote(xb.at[held], rxb.at[held], xb_s.at[0], xb_r.at[g], {"ctx": partner})

    with scope("tw"):
        loads[0].wait()
        loads[1].wait()
    with scope("w"):
        wide_table[...] = jnp.zeros_like(wide_table)
        wide_table[:, : table_ref.shape[1]] = table_ref[...]
        hot = (
            lax.broadcasted_iota(jnp.int32, (table_ref.shape[0], toks), 0) == index_ref[...]
        ).astype(F32)
        w_t = lax.dot_general(
            wide_table[...],
            hot,
            (((0,), (0,)), ((), ())),
            preferred_element_type=F32,
            precision=lax.Precision.HIGHEST,
        )
        wt_ref[...] = w_t
    with scope("cw"):
        loads[2].wait()
        loads[3].wait()
    fill_d.start()
    with scope("bc"):
        b_t = b_ref[...].astype(F32).T.astype(BF16)
        bt_ref[...] = b_t
        c_t = c_ref[...].astype(F32).T
        ct_ref[...] = c_t.astype(BF16)
        for k in range(bits):
            lam_t = w_t[low_bits + 1 + k : low_bits + 2 + k, :]
            rise_t[k * nstate : (k + 1) * nstate, :] = (c_t * lam_t).astype(BF16)
    for n in range(halves):
        with scope(f"xw{n}"):
            fill_x(n).wait()
        with scope(f"s{n}"):
            for q in range(n * wide // WIDTH, (n + 1) * wide // WIDTH):
                cols = slice(q * WIDTH, (q + 1) * WIDTH)
                s_buf[:, :, cols] = mm(b_t, x_ref[:, cols]).reshape(CHUNKS, rows_q, WIDTH)
    with scope("barrier"):
        ends = (col > 0).astype(jnp.int32) + inner.astype(jnp.int32)
        pl.semaphore_wait(barrier, heads + ends)

    for q in range(CHUNKS):
        wanted = inner
        if splits_up(1, q) and q % 2:
            wanted = inner & jnp.logical_not(beside & mine[1])
        pl.when(wanted | (last & mine[0]) if q < EARLY else wanted)(x0_copy(q).start)

    with scope("dw"):
        fill_d.wait()
    with scope("g"):
        for k in reversed(range(bits)):

            @pl.when(is_set[k])
            def _():
                for q in range(strips):
                    cols = slice(q * WIDTH, (q + 1) * WIDTH)
                    part_g = mm(rise_t[k * nstate : (k + 1) * nstate, :], d_ref[:, cols])
                    g_buf[k, :, :, cols] = part_g.reshape(CHUNKS, rows_q, WIDTH)

            if k:

                @pl.when(last)
                def _():
                    for q in range(CHUNKS):
                        if splits_down(k, q):
                            pl.when(mine[1 - q % 2])(pre_copy(k, q).start)
                        elif k == top:
                            back_copy(k, q).start()

            else:
                for q in range(EARLY):
                    pl.when(last & mine[1])(xg_copy(q).start)

                @pl.when(beside & mine[1])
                def _():
                    for q in range(CHUNKS):
                        if splits_down(1, q) and q % 2 == 0:
                            xg_copy(q).start()

    with scope("w2"):
        w_ref[...] = wt_ref[...].T
        carry[...] = jnp.zeros_like(carry)

        @pl.when(last)
        def _():
            tot[...] = jnp.zeros_like(tot)

        pl.when(last & mine[1])(lambda: rxb.__setitem__(..., jnp.zeros_like(rxb)))
        if split:

            @pl.when(beside & mine[1])
            def _():
                for q in range(CHUNKS):
                    if splits_down(1, q) and q % 2:
                        rxb[q] = jnp.zeros_like(rxb[q])

    half = TILE // 2

    def diagonal(w_rows):
        row = lax.broadcasted_iota(jnp.int32, (half, half), 0)
        at = lax.broadcasted_iota(jnp.int32, (half, half), 1)
        differ = row ^ at
        weight = jnp.broadcast_to(w_rows[:, 0:1], (half, half))
        for n in range(tile_bits - 1):
            weight = jnp.where(differ >= 1 << n, w_rows[:, n + 1 : n + 2], weight)
        return jnp.where(at <= row, weight, 0.0)

    def weigh(i):
        rows = slice(i * TILE, (i + 1) * TILE)
        w_rows = w_ref[rows, :]
        upper, lower = w_rows[:half], w_rows[half:]
        side = jnp.broadcast_to(lower[:, tile_bits : tile_bits + 1], (half, half))
        weight = jnp.concatenate(
            [
                jnp.concatenate([diagonal(upper), jnp.zeros((half, half), F32)], axis=1),
                jnp.concatenate([side, diagonal(lower)], axis=1),
            ],
            axis=0,
        )
        c_i, d_i = c_ref[rows, :], d_ref[rows, :]
        for j in range(i + 1):
            cols = slice(j * TILE, (j + 1) * TILE)
            if j < i:
                level = tile_bits + (i ^ j).bit_length()
                factor = w_rows[:, level : level + 1]
            else:
                factor = weight
            mix[rows, cols] = (mm_nt(c_i, b_ref[cols, :]) * factor).astype(BF16)
            d_mix[rows, cols] = (mm_nt(d_i, x_ref[cols, :]) * factor).astype(BF16)

    def near_y(i):
        rows = slice(i * TILE, (i + 1) * TILE)
        seen = slice(0, (i + 1) * TILE)
        y_acc[rows, :] = mm(mix[rows, seen], x_ref[seen, :])
        grads[1, :, rows] = mm_nt(bt_ref[:, seen], d_mix[rows, seen])

    def near_dx(j):
        cols = slice(j * TILE, (j + 1) * TILE)
        seen = slice(j * TILE, toks)
        dx_acc[cols, :] = mm_tn(mix[seen, cols], d_ref[seen, :])
        grads[0, :, cols] = mm(ct_ref[:, seen], d_mix[seen, cols])

    def source(k, q):
        here = low_top[k]
        if k == 1 and splits_up(1, q):
            here = here & jnp.logical_not(beside & mine[1 - q % 2])
            if q % 2 == 0:
                pl.when(beside & mine[1])(x0_copy(q).wait_recv)

        @pl.when(here)
        def _():
            x0_copy(q).wait_recv()
            group = s_buf[q] + rx0[q]
            for j in range(1, k):
                up_copy(j, q).wait_recv()
                group = group + rc[j - 1, q]
            up[q] = group
            up_copy(k, q).start()

    def relay_up(k, q):
        @pl.when(relay[k])
        def _():
            up_copy(k, q).wait_recv()
            when(carried_up(k, q), forward_copy(k, q).start)

    def gather(k, q):
        @pl.when(last & mine[q % 2])
        def _():
            up_copy(k, q).wait_recv()
            gather_copy(k, q).start()

    def descend(k, q):
        if splits_down(k, q):

            @pl.when(last & mine[q % 2])
            def _():
                pre_copy(k, q).wait_recv()
                g_buf[k, q] = g_buf[k, q] + rb[k - 1, q]
                back_copy(k, q).start()

        else:
            pl.when(last)(back_copy(k, q).start)

    def relay_down(k, q):
        @pl.when(relay[k])
        def _():
            def add():
                back_copy(k, q).wait_recv()
                g_buf[k, q] = g_buf[k, q] + rb[k - 1, q]

            when(carried_down(k, q), add)
            back_copy(k, q).start()

    def cross(q):
        @pl.when(mine[1])
        def _():
            xb[q] = tot[q] + g_buf[0, q]

        @pl.when(mine[0])
        def _():
            xb[q] = tot[q]

    def pass_down(k, q):
        here = low_top[k] & jnp.logical_not(beside) if split else low_top[k]

        @pl.when(here)
        def _():
            back_copy(k, q).wait_recv()
            got = rb[k - 1, q]
            tot[q] = got
            for j in range(1, k):
                g_buf[j, q] = g_buf[j, q] + got
                back_copy(j, q).start()
            cross(q)
            xb_copy(q).start()

    def beside_down(q):
        def own():
            back_copy(1, q).wait_recv()
            tot[q] = rb[0, q]
            cross(q)
            xb_copy(q).start()

        if splits_down(1, q):
            pl.when(beside & mine[q % 2])(own)

            @pl.when(beside & mine[1 - q % 2])
            def _():
                tot[q] = jnp.zeros_like(tot[q])

        else:
            pl.when(beside)(own)

    def spread(array, g):
        n0, n1 = GROUPS[g][0] * rows_q, GROUPS[g][1] * rows_q
        copies = []
        for m, peer in enumerate(peers):
            lanes = pl.ds(pl.multiple_of(peer * part, part), part)
            copies.append(
                remote(
                    grads.at[array, pl.ds(n0, n1 - n0), lanes],
                    hr.at[m, array, pl.ds(n0, n1 - n0)],
                    hd_s.at[0],
                    hd_r.at[array, g],
                    {"head": peer},
                )
            )
        return copies

    def far_up(g):
        q0, q1 = GROUPS[g]
        n0, n1 = q0 * rows_q, q1 * rows_q
        for q in range(q0, q1):
            pl.when(last & mine[1])(x0_copy(q).wait_recv)
            for k in levels:
                if splits_up(k, q):
                    pl.when(last & mine[1 - q % 2])(gather_copy(k, q).wait_recv)
                else:
                    pl.when(last)(up_copy(k, q).wait_recv)
        for k in range(bits):

            @pl.when(is_set[k])
            def _():
                got = rc[k - 1, q0:q1] if k else rx0[q0:q1]
                carry[k * nstate + n0 : k * nstate + n1, :] = got.reshape(n1 - n0, feats).astype(BF16)

        held = [carry[k * nstate + n0 : k * nstate + n1, :] for k in range(bits)]
        terms = mm_nt(jnp.concatenate(held, axis=0), d_ref[...])
        total = grads[1, n0:n1, :]
        for k in range(bits):
            lam = wt_ref[low_bits + 1 + k : low_bits + 2 + k, :]
            total = total + terms[k * (n1 - n0) : (k + 1) * (n1 - n0), :] * lam
        grads[1, n0:n1, :] = total
        for copy in spread(1, g):
            copy.start()

    def far_down(g):
        q0, q1 = GROUPS[g]
        n0, n1 = q0 * rows_q, q1 * rows_q
        pl.when(mine[0] | jnp.logical_not(last | beside) if split else mine[0] | inner)(
            xb_all(q0, q1 - q0, g).wait_recv
        )
        if split:
            given = sum(not splits_down(1, q) or q % 2 == 0 for q in range(q0, q1))
            pl.when(beside & mine[1])(xb_all(q0, given, g).wait_recv)
        held = (tot[q0:q1] + rxb[q0:q1]).reshape(n1 - n0, feats).astype(BF16)
        back[n0:n1, :] = held
        grads[0, n0:n1, :] = grads[0, n0:n1, :] + mm_nt(held, x_ref[...])
        for copy in spread(0, g):
            copy.start()

    def late_sends(q):
        pl.when(last & mine[0])(x0_copy(q).start)
        pl.when(last & mine[1])(xg_copy(q).start)

    def rises():
        c_f = c_ref[...].astype(F32)
        for k in range(bits):
            lam = w_ref[:, low_bits + 1 + k : low_bits + 2 + k]
            rise[:, k * nstate : (k + 1) * nstate] = (c_f * lam).astype(BF16)

    plan = []

    def put(time, name, step, *args):
        plan.append((time, len(plan), name, step, args))

    def rise_at(k, q):
        return (6.4 if k == 1 else 9.1 + 5.8 * (k - 2)) + BEAT * q

    def fall_at(k, q):
        return 10.6 + 3.4 * (top - k) + BEAT * q

    for q in range(CHUNKS):
        for k in levels:
            put(rise_at(k, q), "source", source, k, q)
            put(fall_at(k, q), "pass_down", pass_down, k, q)
            if k > 1:
                put(rise_at(k, q) + 2.9, "relay_up", relay_up, k, q)
                put(7.1 + BEAT * q if k == top else fall_at(k, q) - 1.4, "relay_down", relay_down, k, q)
            if splits_up(k, q):
                put(rise_at(k, q) + 3.1, "gather", gather, k, q)
            if k < top:
                put(9.4 + 0.28 * q, "descend", descend, k, q)
            elif splits_down(k, q):
                put(8.4 + 0.2 * (q - TOP_SPLIT[0]), "descend", descend, k, q)
        if split:
            put(17.0 + 0.45 * q, "beside", beside_down, q)
        if q >= EARLY:
            put(8.0 + 0.95 * (q - EARLY), "late", late_sends, q)
    deeper = max(top - 2, 0)
    for g, (up_at, down_at) in enumerate(FAR_AT):
        put(up_at + 5.8 * deeper, "far_up", far_up, g)
        put(down_at + 3.4 * deeper, "far_down", far_down, g)
    near = [(weigh, 0)]
    for i in range(1, blocks):
        near += [(weigh, i), (near_y, i - 1)]
    near += [(near_y, blocks - 1)] + [(near_dx, j) for j in range(blocks)]
    for n, (step, i) in enumerate(near):
        put(4.6 + 13.5 / len(near) * n, step.__name__, step, i)
    put(20.0, "rises", rises)
    for _, _, name, step, args in sorted(plan, key=lambda item: item[:2]):
        with scope(name + "_" + "_".join(str(a) for a in args)):
            step(*args)

    with scope("y"):
        for q in range(strips):
            cols = slice(q * WIDTH, (q + 1) * WIDTH)
            y_ref[:, cols] = (y_acc[:, cols] + mm(rise[...], carry[:, cols])).astype(BF16)
    with scope("dx"):
        for q in range(strips):
            cols = slice(q * WIDTH, (q + 1) * WIDTH)
            dx_ref[:, cols] = (dx_acc[:, cols] + mm(b_ref[...], back[:, cols])).astype(BF16)
    own = pl.ds(pl.multiple_of(head * part, part), part)
    for g, (q0, q1) in enumerate(GROUPS):
        rows = pl.ds(q0 * rows_q, (q1 - q0) * rows_q)
        for array in (1, 0):
            with scope(f"heads_{g}_{array}"):
                total = grads[array, rows, own]
                if heads > 1:
                    given = hr.at[:, array, rows]
                    remote(given, given, hd_s.at[0], hd_r.at[array, g], {"head": peers[0]}).wait_recv()
                    for m in range(heads - 1):
                        total = total + hr[m, array, rows]
                (db_ref, dc_ref)[array][:, rows] = total.T

    def sent(sem, n, condition):
        if n:
            held = s_buf.at[pl.ds(0, n)]
            pl.when(condition)(remote(held, held, sem, x0_r.at[0], {"ctx": partner}).wait_send)

    with scope("drain"):
        if heads > 1:
            remote(hr, hr, hd_s.at[0], hd_r.at[0, 0], {"head": peers[0]}).wait_send()
        if split:
            apart = jnp.logical_not(beside)
            sent(x0_s.at[0], CHUNKS, (inner & apart) | mine[0])
            sent(x0_s.at[0], owned(splits_up, 1, 0), beside & mine[1])
            sent(xb_s.at[0], CHUNKS, (inner & apart) | mine[1])
            sent(xb_s.at[0], owned(splits_down, 1, 0), beside & mine[0])
        else:
            sent(x0_s.at[0], CHUNKS, inner | mine[0])
            sent(xb_s.at[0], CHUNKS, inner | mine[1])
        for k in levels:
            for line in range(2):
                full = mine[line] & jnp.logical_not(beside)
                edge = mine[line] & beside
                sent(up_s.at[0], CHUNKS, low_top[k] & full)
                sent(up_s.at[0], owned(splits_up, k, line), low_top[k] & edge)
                sent(fw_s.at[k - 1], CHUNKS, relay[k] & full)
                sent(fw_s.at[k - 1], owned(splits_up, k, line), relay[k] & edge)
                sent(ga_s.at[k - 1], shared(splits_up, k, line), last & mine[line])
                sent(pr_s.at[k - 1], shared(splits_down, k, 1 - line), last & mine[line])
                sent(bk_s.at[k - 1], CHUNKS, is_set[k] & mine[line] & inner)
                sent(bk_s.at[k - 1], owned(splits_down, k, line), last & mine[line])


def write_out(*refs):
    copies = [pltpu.make_async_copy(refs[n], refs[n + 4], refs[8].at[n]) for n in range(4)]
    for copy in copies:
        copy.start()
    for copy in copies:
        copy.wait()


def local(x_in, b_in, c_in, d_out, table, level_index):
    toks, feats = x_in.shape
    nstate = b_in.shape[1]
    count, heads = lax.axis_size("ctx"), lax.axis_size("head")
    bits = count.bit_length() - 1
    strips = feats // WIDTH
    index = level_index.reshape(1, toks)
    rows = toks // heads
    ups = max(bits - 1, 1)
    others = max(heads - 1, 1)
    vmem = pl.BlockSpec(memory_space=pltpu.VMEM)
    hbm = pl.BlockSpec(memory_space=pltpu.HBM)
    dma = pltpu.SemaphoreType.DMA
    slab = (CHUNKS, nstate // CHUNKS, feats)
    results = pl.pallas_call(
        functools.partial(kernel, count, heads),
        out_shape=(
            pltpu.VMEM((toks, feats), BF16),
            pltpu.VMEM((toks, feats), BF16),
            pltpu.VMEM((rows, nstate), F32),
            pltpu.VMEM((rows, nstate), F32),
        ),
        in_specs=[hbm] * 6,
        out_specs=(vmem,) * 4,
        scratch_shapes=[
            pltpu.VMEM((toks, feats), BF16),
            pltpu.VMEM((toks, feats), BF16),
            pltpu.VMEM((toks, nstate), BF16),
            pltpu.VMEM((toks, nstate), BF16),
            pltpu.VMEM(table.shape, F32),
            pltpu.VMEM((1, toks), jnp.int32),
            pltpu.VMEM((table.shape[0], nstate), F32),
            pltpu.VMEM((toks, nstate), F32),
            pltpu.VMEM((nstate, toks), F32),
            pltpu.VMEM((nstate, toks), BF16),
            pltpu.VMEM((nstate, toks), BF16),
            pltpu.VMEM((toks, toks), BF16),
            pltpu.VMEM((toks, toks), BF16),
            pltpu.VMEM((toks, feats), F32),
            pltpu.VMEM((toks, feats), F32),
            pltpu.VMEM((2, nstate, toks), F32),
            pltpu.VMEM((toks, bits * nstate), BF16),
            pltpu.VMEM((bits * nstate, toks), BF16),
            pltpu.VMEM((bits * nstate, feats), BF16),
            pltpu.VMEM((nstate, feats), BF16),
            pltpu.VMEM(slab, F32),
            pltpu.VMEM((bits,) + slab, F32),
            pltpu.VMEM(slab, F32),
            pltpu.VMEM(slab, F32),
            pltpu.VMEM((ups,) + slab, F32),
            pltpu.VMEM((ups,) + slab, F32),
            pltpu.VMEM(slab, F32),
            pltpu.VMEM(slab, F32),
            pltpu.VMEM(slab, F32),
            pltpu.VMEM((others, 2, nstate, rows), F32),
            dma((4,)),
            dma((2,)),
            dma((1,)),
            dma((1,)),
            dma((CHUNKS,)),
            dma((1,)),
            dma((ups,)),
            dma((ups, CHUNKS)),
            dma((ups,)),
            dma((ups,)),
            dma((ups,)),
            dma((ups, CHUNKS)),
            dma((1,)),
            dma((len(GROUPS),)),
            dma((1,)),
            dma((2, len(GROUPS))),
        ],
        compiler_params=pltpu.CompilerParams(
            collective_id=0,
            has_side_effects=True,
            vmem_limit_bytes=VMEM_BYTES - 4 * toks * feats - 8 * rows * nstate - SPARE,
        ),
    )(x_in, b_in, c_in, d_out, table, index)
    return pl.pallas_call(
        write_out,
        out_shape=tuple(jax.ShapeDtypeStruct(r.shape, r.dtype) for r in results),
        in_specs=[vmem] * 4,
        out_specs=(hbm,) * 4,
        scratch_shapes=[dma((4,))],
        compiler_params=pltpu.CompilerParams(vmem_limit_bytes=1024 * 1024),
    )(*results)


def solution(mesh):
    return jax.shard_map(
        local,
        mesh=mesh,
        in_specs=(
            P("ctx", "head"),
            P("ctx", None),
            P("ctx", None),
            P("ctx", "head"),
            P(),
            P("ctx"),
        ),
        out_specs=(
            P("ctx", "head"),
            P("ctx", "head"),
            P(("ctx", "head"), None),
            P(("ctx", "head"), None),
        ),
        check_vma=False,
    )
```

time: 46.3 us -> 40.3 us (0.87)
  Pallas kernels: 45.2 us -> 39.3 us
    pallas_call x1, Pallas kernels: 43.1 us -> 37.2 us  [local(): pl.pallas_call(functools.partial(kernel, count, heads), out_shape=(pltpu....]
where the time goes in v1:
time: 40.3 us; the launch traced here: 40.1 us
  Pallas kernels  39.3 us (98%)
  between operations  0.8 us (2%)
    pallas_call x1, Pallas kernels, local(): pl.pallas_call(functools.partial(kernel, count, heads), out_shape=(pltpu....  37.2 us
    pallas_call x1, Pallas kernels, local(): pl.pallas_call(write_out, out_shape=tuple((jax.ShapeDtypeStruct(r.shape,...  2.11 us

profile of v1, /device:TPU:0, one launch (start us, length us, event | category | flops | bytes accessed | tf_op | source)
XLA Modules:
  0.0 40.1 jit_solution(11064712516193576538)
XLA Ops:
  0.6 37.2 %shard_map.93 = (bf16[1024,1024]{1,0:T(8,128)(2,1)S(1)}, bf16[1024,1024]{1,0:T(8,128)(2,1)S(1)}, f32[256,128]{1,0:T(8,128)S(1)}, f32[256,128]{1,0:T(8,128)S(1)}) custom-call(bf16[1024,1024]{1,0:T(8,128)(2,1)} %x_hbm.1, bf16[1024,128]{1,0:T(8,128)(2,1)} %b_hbm.1, bf16[1024,128]{1,0:T(8,128)(2,1)} %c_hbm.1, bf16[1024,1024]{1,0:T(8,128)(2,1)} %d_hbm.1, ...), custom_call_target="tpu_custom_call" | custom-call | tf_op jit(solution)/shard_map/pallas_call | solution.py:667
  37.8 2.1 %shard_map.94 = (bf16[1024,1024]{1,0:T(8,128)(2,1)}, bf16[1024,1024]{1,0:T(8,128)(2,1)}, f32[256,128]{1,0:T(8,128)}, f32[256,128]{1,0:T(8,128)}) custom-call(bf16[1024,1024]{1,0:T(8,128)(2,1)S(1)} %get-tuple-element.8.refs_0_, bf16[1024,1024]{1,0:T(8,128)(2,1)S(1)} %get-tuple-element.9.refs_1_, f32[256,128]{1,0:T(8,128)S(1)} %get-tuple-element.10.refs_2_, ...), custom_call_target="tpu_custom_call" | custom-call | tf_op jit(solution)/shard_map/pallas_call | solution.py:731

commit v2 on v1

--- a/solution.py
+++ b/solution.py
@@ -15,10 +15,12 @@
 WIDTH = 256
 CHUNKS = 16
 GROUPS = ((0, 8), (8, 14), (14, 16))
-FAR_AT = ((21.5, 22.9), (25.3, 26.6), (26.8, 28.0))
+FIRST_AT = ((13.5, 16.6, 18.4), (22.6, 26.5, 28.0), (16.9, 19.9), (25.2, 27.6), (19.3, 20.7))
+INNER_AT = ((18.9, 22.3, 23.5), (24.0, 26.5, 28.0), (21.9, 25.2), (26.3, 27.6), (24.4, 25.5))
+LAST_AT = ((24.0, 27.2, 28.8), (23.0, 25.8, 27.9), (25.9, 28.7), (25.5, 28.4), (29.6, 30.2))
 EARLY = 2
 BEAT = 0.7
-UP_SPLIT = range(1, 15)
+UP_SPLIT = range(4, 16)
 DOWN_SPLIT = range(1, 11)
 TOP_SPLIT = range(12, 16)
 VMEM_BYTES = 67043328
@@ -91,6 +93,8 @@
     xb,
     rxb,
     hr,
+    h1,
+    sums,
     small_sem,
     x_sem,
     d_sem,
@@ -107,6 +111,7 @@
     xb_r,
     hd_s,
     hd_r,
+    h1_r,
 ):
     bits = count.bit_length() - 1
     top = bits - 1
@@ -146,6 +151,9 @@
     def shared(splits, k, line):
         return sum(splits(k, q) and q % 2 == line for q in range(CHUNKS))
 
+    first = col == 0
+    classes = (first & inner, inner & jnp.logical_not(first), last)
+
     def carried_up(k, q):
         return jnp.logical_not(beside) | mine[q % 2] if splits_up(k, q) else None
 
@@ -170,7 +178,7 @@
             )
         )
     ]
-    halves = 2
+    halves = 4
     wide = feats // halves
 
     def fill_x(n):
@@ -178,10 +186,24 @@
         return pltpu.make_async_copy(x_hbm.at[:, cols], x_ref.at[:, cols], x_sem.at[n])
 
     fill_d = pltpu.make_async_copy(d_hbm, d_ref, d_sem.at[0])
-    for load in loads:
-        load.start()
-    for n in range(halves):
-        fill_x(n).start()
+    def load_states():
+        loads[3].start()
+        for n in range(halves):
+            fill_x(n).start()
+
+    def load_weights():
+        for load in loads[:3]:
+            load.start()
+
+    @pl.when(inner)
+    def _():
+        load_states()
+        load_weights()
+
+    @pl.when(last)
+    def _():
+        load_weights()
+        fill_d.start()
 
     barrier = pltpu.get_barrier_semaphore()
     pl.semaphore_signal(barrier, inc=1, device_id={"ctx": partner}, device_id_type=MESH)
@@ -211,6 +233,9 @@
     def x0_copy(q):
         return remote(s_buf.at[q], rx0.at[q], x0_s.at[0], x0_r.at[q], {"ctx": partner})
 
+    def fall_sem(k, q):
+        return rb_r.at[k - 2, q] if k > 1 else rc_r.at[0, q]
+
     def up_copy(k, q):
         return remote(up.at[q], rc.at[k - 1, q], up_s.at[0], rc_r.at[k - 1, q], {"ctx": me + 2})
 
@@ -224,12 +249,12 @@
 
     def pre_copy(k, q):
         return remote(
-            g_buf.at[k, q], rb.at[k - 1, q], pr_s.at[k - 1], rb_r.at[k - 1, q], {"ctx": partner}
+            g_buf.at[k, q], rb.at[k - 1, q], pr_s.at[k - 1], fall_sem(k if k > 1 else top, q), {"ctx": partner}
         )
 
     def back_copy(k, q):
         return remote(
-            g_buf.at[k, q], rb.at[k - 1, q], bk_s.at[k - 1], rb_r.at[k - 1, q], {"ctx": me - 2}
+            g_buf.at[k, q], rb.at[k - 1, q], bk_s.at[k - 1], fall_sem(k, q), {"ctx": me - 2}
         )
 
     def group_of(q):
@@ -247,10 +272,19 @@
         held = pl.ds(q0, n)
         return remote(xb.at[held], rxb.at[held], xb_s.at[0], xb_r.at[g], {"ctx": partner})
 
-    with scope("tw"):
-        loads[0].wait()
-        loads[1].wait()
-    with scope("w"):
+    def states():
+        with scope("b"):
+            b_t = b_ref[...].astype(F32).T.astype(BF16)
+            bt_ref[...] = b_t
+        with scope("xw"):
+            for n in range(halves):
+                fill_x(n).wait()
+        with scope("s"):
+            for n in range(halves):
+                cols = slice(n * wide, (n + 1) * wide)
+                s_buf[:, :, cols] = mm(b_t, x_ref[:, cols]).reshape(CHUNKS, rows_q, wide)
+
+    def weights():
         wide_table[...] = jnp.zeros_like(wide_table)
         wide_table[:, : table_ref.shape[1]] = table_ref[...]
         hot = (
@@ -264,39 +298,48 @@
             precision=lax.Precision.HIGHEST,
         )
         wt_ref[...] = w_t
-    with scope("cw"):
-        loads[2].wait()
-        loads[3].wait()
-    fill_d.start()
-    with scope("bc"):
-        b_t = b_ref[...].astype(F32).T.astype(BF16)
-        bt_ref[...] = b_t
         c_t = c_ref[...].astype(F32).T
         ct_ref[...] = c_t.astype(BF16)
         for k in range(bits):
             lam_t = w_t[low_bits + 1 + k : low_bits + 2 + k, :]
             rise_t[k * nstate : (k + 1) * nstate, :] = (c_t * lam_t).astype(BF16)
-    for n in range(halves):
-        with scope(f"xw{n}"):
-            fill_x(n).wait()
-        with scope(f"s{n}"):
-            for q in range(n * wide // WIDTH, (n + 1) * wide // WIDTH):
-                cols = slice(q * WIDTH, (q + 1) * WIDTH)
-                s_buf[:, :, cols] = mm(b_t, x_ref[:, cols]).reshape(CHUNKS, rows_q, WIDTH)
-    with scope("barrier"):
+
+    def meet():
         ends = (col > 0).astype(jnp.int32) + inner.astype(jnp.int32)
         pl.semaphore_wait(barrier, heads + ends)
 
-    for q in range(CHUNKS):
-        wanted = inner
-        if splits_up(1, q) and q % 2:
-            wanted = inner & jnp.logical_not(beside & mine[1])
-        pl.when(wanted | (last & mine[0]) if q < EARLY else wanted)(x0_copy(q).start)
+    @pl.when(inner)
+    def _():
+        with scope("bw"):
+            loads[3].wait()
+        fill_d.start()
+        states()
+        with scope("barrier"):
+            meet()
+        for q in range(CHUNKS):
+            if splits_up(1, q) and q % 2:
+                pl.when(jnp.logical_not(beside & mine[1]))(x0_copy(q).start)
+            else:
+                x0_copy(q).start()
+        with scope("tw"):
+            for load in loads[:3]:
+                load.wait()
+        with scope("w"):
+            weights()
+
+    @pl.when(last)
+    def _():
+        with scope("tw"):
+            for load in loads[:3]:
+                load.wait()
+        load_states()
+        with scope("w"):
+            weights()
 
     with scope("dw"):
         fill_d.wait()
-    with scope("g"):
-        for k in reversed(range(bits)):
+    for k in reversed(range(bits)):
+        with scope(f"g{k}"):
 
             @pl.when(is_set[k])
             def _():
@@ -305,25 +348,33 @@
                     part_g = mm(rise_t[k * nstate : (k + 1) * nstate, :], d_ref[:, cols])
                     g_buf[k, :, :, cols] = part_g.reshape(CHUNKS, rows_q, WIDTH)
 
-            if k:
-
-                @pl.when(last)
-                def _():
-                    for q in range(CHUNKS):
-                        if splits_down(k, q):
-                            pl.when(mine[1 - q % 2])(pre_copy(k, q).start)
-                        elif k == top:
-                            back_copy(k, q).start()
-
-            else:
+        @pl.when(last)
+        def _():
+            if k == top:
+                meet()
+            for q in range(CHUNKS if k else 0):
+                if splits_down(k, q):
+                    pl.when(mine[1 - q % 2])(pre_copy(k, q).start)
+                elif k == top:
+                    back_copy(k, q).start()
+            if k == 0:
                 for q in range(EARLY):
-                    pl.when(last & mine[1])(xg_copy(q).start)
-
-                @pl.when(beside & mine[1])
-                def _():
-                    for q in range(CHUNKS):
-                        if splits_down(1, q) and q % 2 == 0:
-                            xg_copy(q).start()
+                    pl.when(mine[1])(xg_copy(q).start)
+
+        if k == 0:
+
+            @pl.when(beside & mine[1])
+            def _():
+                for q in range(CHUNKS):
+                    if splits_down(1, q) and q % 2 == 0:
+                        xg_copy(q).start()
+
+    @pl.when(last)
+    def _():
+        loads[3].wait()
+        states()
+        for q in range(EARLY):
+            pl.when(mine[0])(x0_copy(q).start)
 
     with scope("w2"):
         w_ref[...] = wt_ref[...].T
@@ -479,63 +530,121 @@
         else:
             pl.when(beside)(own)
 
+    final = len(GROUPS) - 1
+    pair = head % 2
+    fellow = head + 1 - 2 * pair
+    ways = heads // 2
+
+    def lanes_of(h):
+        return pl.ds(pl.multiple_of(h * part, part), part)
+
+    def rows_of(g):
+        return pl.ds(GROUPS[g][0] * rows_q, (GROUPS[g][1] - GROUPS[g][0]) * rows_q)
+
     def spread(array, g):
-        n0, n1 = GROUPS[g][0] * rows_q, GROUPS[g][1] * rows_q
-        copies = []
-        for m, peer in enumerate(peers):
-            lanes = pl.ds(pl.multiple_of(peer * part, part), part)
-            copies.append(
+        rows = rows_of(g)
+        if g == final:
+            for m, peer in enumerate(peers):
                 remote(
-                    grads.at[array, pl.ds(n0, n1 - n0), lanes],
-                    hr.at[m, array, pl.ds(n0, n1 - n0)],
+                    grads.at[array, rows, lanes_of(peer)],
+                    hr.at[m, array, rows],
                     hd_s.at[0],
                     hd_r.at[array, g],
                     {"head": peer},
-                )
-            )
-        return copies
-
-    def far_up(g):
+                ).start()
+        else:
+            for j in range(ways):
+                remote(
+                    grads.at[array, rows, lanes_of(2 * j + 1 - pair)],
+                    h1.at[j, array, rows],
+                    hd_s.at[1],
+                    h1_r.at[array, g],
+                    {"head": fellow},
+                ).start()
+
+    def middle(array, g):
+        rows = rows_of(g)
+        if ways:
+            given = h1.at[:, array, rows]
+            remote(given, given, hd_s.at[1], h1_r.at[array, g], {"head": fellow}).wait_recv()
+        for m in range(max(ways, 1)):
+            j = (head // 2 + m) % max(ways, 1)
+            total = grads[array, rows, lanes_of(2 * j + pair)]
+            if ways:
+                total = total + h1[j, array, rows]
+            sums[m, array, rows] = total
+            if m:
+                remote(
+                    sums.at[m, array, rows],
+                    hr.at[m - 1, array, rows],
+                    hd_s.at[2],
+                    hd_r.at[array, g],
+                    {"head": 2 * j + pair},
+                ).start()
+
+    def far_up(g, which):
+        ending = which == 2
         q0, q1 = GROUPS[g]
         n0, n1 = q0 * rows_q, q1 * rows_q
-        for q in range(q0, q1):
-            pl.when(last & mine[1])(x0_copy(q).wait_recv)
-            for k in levels:
-                if splits_up(k, q):
-                    pl.when(last & mine[1 - q % 2])(gather_copy(k, q).wait_recv)
-                else:
-                    pl.when(last)(up_copy(k, q).wait_recv)
-        for k in range(bits):
-
-            @pl.when(is_set[k])
-            def _():
-                got = rc[k - 1, q0:q1] if k else rx0[q0:q1]
-                carry[k * nstate + n0 : k * nstate + n1, :] = got.reshape(n1 - n0, feats).astype(BF16)
-
-        held = [carry[k * nstate + n0 : k * nstate + n1, :] for k in range(bits)]
-        terms = mm_nt(jnp.concatenate(held, axis=0), d_ref[...])
-        total = grads[1, n0:n1, :]
-        for k in range(bits):
-            lam = wt_ref[low_bits + 1 + k : low_bits + 2 + k, :]
-            total = total + terms[k * (n1 - n0) : (k + 1) * (n1 - n0), :] * lam
-        grads[1, n0:n1, :] = total
-        for copy in spread(1, g):
-            copy.start()
-
-    def far_down(g):
+
+        @pl.when(classes[which])
+        def _():
+            for q in range(q0, q1) if ending else ():
+                pl.when(mine[1])(x0_copy(q).wait_recv)
+                for k in levels:
+                    if splits_up(k, q):
+                        pl.when(mine[1 - q % 2])(gather_copy(k, q).wait_recv)
+                    else:
+                        up_copy(k, q).wait_recv()
+            for k in range(bits):
+
+                @pl.when(is_set[k])
+                def _():
+                    got = rc[k - 1, q0:q1] if k else rx0[q0:q1]
+                    carry[k * nstate + n0 : k * nstate + n1, :] = got.reshape(
+                        n1 - n0, feats
+                    ).astype(BF16)
+
+            held = [carry[k * nstate + n0 : k * nstate + n1, :] for k in range(bits)]
+            terms = mm_nt(jnp.concatenate(held, axis=0), d_ref[...])
+            total = grads[1, n0:n1, :]
+            for k in range(bits):
+                lam = wt_ref[low_bits + 1 + k : low_bits + 2 + k, :]
+                total = total + terms[k * (n1 - n0) : (k + 1) * (n1 - n0), :] * lam
+            grads[1, n0:n1, :] = total
+            spread(1, g)
+
+    def far_down(g, which):
+        ending = which == 2
         q0, q1 = GROUPS[g]
         n0, n1 = q0 * rows_q, q1 * rows_q
-        pl.when(mine[0] | jnp.logical_not(last | beside) if split else mine[0] | inner)(
-            xb_all(q0, q1 - q0, g).wait_recv
-        )
-        if split:
-            given = sum(not splits_down(1, q) or q % 2 == 0 for q in range(q0, q1))
-            pl.when(beside & mine[1])(xb_all(q0, given, g).wait_recv)
-        held = (tot[q0:q1] + rxb[q0:q1]).reshape(n1 - n0, feats).astype(BF16)
-        back[n0:n1, :] = held
-        grads[0, n0:n1, :] = grads[0, n0:n1, :] + mm_nt(held, x_ref[...])
-        for copy in spread(0, g):
-            copy.start()
+
+        @pl.when(classes[which])
+        def _():
+            every = xb_all(q0, q1 - q0, g).wait_recv
+            if ending:
+                pl.when(mine[0])(every)
+            elif split:
+                pl.when(mine[0] | jnp.logical_not(beside))(every)
+                given = sum(not splits_down(1, q) or q % 2 == 0 for q in range(q0, q1))
+                pl.when(beside & mine[1])(xb_all(q0, given, g).wait_recv)
+            else:
+                every()
+            held = (tot[q0:q1] + rxb[q0:q1]).reshape(n1 - n0, feats).astype(BF16)
+            back[n0:n1, :] = held
+            grads[0, n0:n1, :] = grads[0, n0:n1, :] + mm_nt(held, x_ref[...])
+            spread(0, g)
+
+    def halfway(array, g, which, turn=None):
+        here = classes[which] if turn is None else classes[which] & (pair == turn)
+        pl.when(here)(lambda: middle(array, g))
+
+    def finish_y(n, which):
+        @pl.when(classes[which])
+        def _():
+            for q in range(n * strips // 2, (n + 1) * strips // 2):
+                cols = slice(q * WIDTH, (q + 1) * WIDTH)
+                y_ref[:, cols] = (y_acc[:, cols] + mm(rise[...], carry[:, cols])).astype(BF16)
 
     def late_sends(q):
         pl.when(last & mine[0])(x0_copy(q).start)
@@ -553,63 +662,86 @@
         plan.append((time, len(plan), name, step, args))
 
     def rise_at(k, q):
-        return (6.4 if k == 1 else 9.1 + 5.8 * (k - 2)) + BEAT * q
+        return (6.2 if k == 1 else 9.0 + 5.8 * (k - 2)) + BEAT * q
+
+    def lead(q):
+        n = TOP_SPLIT[0]
+        return BEAT * q if q < n else BEAT * n + 0.4 * (q - n)
 
     def fall_at(k, q):
-        return 10.6 + 3.4 * (top - k) + BEAT * q
+        return 10.2 + 3.6 * (top - k) + lead(q)
 
     for q in range(CHUNKS):
         for k in levels:
             put(rise_at(k, q), "source", source, k, q)
             put(fall_at(k, q), "pass_down", pass_down, k, q)
             if k > 1:
-                put(rise_at(k, q) + 2.9, "relay_up", relay_up, k, q)
-                put(7.1 + BEAT * q if k == top else fall_at(k, q) - 1.4, "relay_down", relay_down, k, q)
+                put(rise_at(k, q) + 3.4, "relay_up", relay_up, k, q)
+                put(6.4 + lead(q) if k == top else fall_at(k, q) - 1.4, "relay_down", relay_down, k, q)
             if splits_up(k, q):
-                put(rise_at(k, q) + 3.1, "gather", gather, k, q)
+                put(rise_at(k, q) + 3.6 + 0.1 * q, "gather", gather, k, q)
             if k < top:
-                put(9.4 + 0.28 * q, "descend", descend, k, q)
+                put(8.4 + 0.28 * q, "descend", descend, k, q)
             elif splits_down(k, q):
-                put(8.4 + 0.2 * (q - TOP_SPLIT[0]), "descend", descend, k, q)
+                put(6.9 + 0.2 * (q - TOP_SPLIT[0]), "descend", descend, k, q)
         if split:
-            put(17.0 + 0.45 * q, "beside", beside_down, q)
+            put(16.0 + 0.45 * q, "beside", beside_down, q)
         if q >= EARLY:
             put(8.0 + 0.95 * (q - EARLY), "late", late_sends, q)
     deeper = max(top - 2, 0)
-    for g, (up_at, down_at) in enumerate(FAR_AT):
-        put(up_at + 5.8 * deeper, "far_up", far_up, g)
-        put(down_at + 3.4 * deeper, "far_down", far_down, g)
+    for which, times in enumerate((FIRST_AT, INNER_AT, LAST_AT)):
+        ups, downs, up_halves, down_halves, ys = times
+        later = 5.8 * deeper
+        for g in range(len(GROUPS)):
+            put(ups[g] + later, "far_up", far_up, g, which)
+            put(downs[g] + later, "far_down", far_down, g, which)
+            if g != final:
+                put(up_halves[g] + later, "halfway", halfway, 1, g, which)
+                if g == final - 1:
+                    put(down_halves[g] + later, "halfway", halfway, 0, g, which, 0)
+                    put(max(down_halves[g], downs[final]) + 0.1 + later, "halfway", halfway, 0, g, which, 1)
+                else:
+                    put(down_halves[g] + later, "halfway", halfway, 0, g, which)
+        for n in range(2):
+            put(ys[n] + later, "finish_y", finish_y, n, which)
     near = [(weigh, 0)]
     for i in range(1, blocks):
         near += [(weigh, i), (near_y, i - 1)]
     near += [(near_y, blocks - 1)] + [(near_dx, j) for j in range(blocks)]
     for n, (step, i) in enumerate(near):
-        put(4.6 + 13.5 / len(near) * n, step.__name__, step, i)
-    put(20.0, "rises", rises)
+        put(4.3 + 13.2 / len(near) * n, step.__name__, step, i)
+    put(18.6, "rises", rises)
     for _, _, name, step, args in sorted(plan, key=lambda item: item[:2]):
         with scope(name + "_" + "_".join(str(a) for a in args)):
             step(*args)
 
-    with scope("y"):
-        for q in range(strips):
-            cols = slice(q * WIDTH, (q + 1) * WIDTH)
-            y_ref[:, cols] = (y_acc[:, cols] + mm(rise[...], carry[:, cols])).astype(BF16)
     with scope("dx"):
         for q in range(strips):
             cols = slice(q * WIDTH, (q + 1) * WIDTH)
             dx_ref[:, cols] = (dx_acc[:, cols] + mm(b_ref[...], back[:, cols])).astype(BF16)
-    own = pl.ds(pl.multiple_of(head * part, part), part)
-    for g, (q0, q1) in enumerate(GROUPS):
-        rows = pl.ds(q0 * rows_q, (q1 - q0) * rows_q)
-        for array in (1, 0):
-            with scope(f"heads_{g}_{array}"):
-                total = grads[array, rows, own]
-                if heads > 1:
-                    given = hr.at[:, array, rows]
-                    remote(given, given, hd_s.at[0], hd_r.at[array, g], {"head": peers[0]}).wait_recv()
-                    for m in range(heads - 1):
-                        total = total + hr[m, array, rows]
-                (db_ref, dc_ref)[array][:, rows] = total.T
+    def finish(array):
+        parts = []
+        for g in range(len(GROUPS)):
+            rows = rows_of(g)
+            if g == final:
+                ahead, total = heads - 1, grads[array, rows, lanes_of(head)]
+            else:
+                ahead, total = max(ways - 1, 0), sums[0, array, rows]
+            if ahead:
+                given = hr.at[pl.ds(0, ahead), array, rows]
+                remote(given, given, hd_s.at[0], hd_r.at[array, g], {"head": fellow}).wait_recv()
+            for m in range(ahead):
+                total = total + hr[m, array, rows]
+            parts.append(total)
+        (db_ref, dc_ref)[array][...] = jnp.concatenate(parts, axis=0).T
+
+    for ending in range(2):
+
+        @pl.when(last if ending else inner)
+        def _():
+            for array in (0, 1) if ending else (1, 0):
+                with scope(f"heads_{array}_{ending}"):
+                    finish(array)
 
     def sent(sem, n, condition):
         if n:
@@ -617,8 +749,14 @@
             pl.when(condition)(remote(held, held, sem, x0_r.at[0], {"ctx": partner}).wait_send)
 
     with scope("drain"):
-        if heads > 1:
-            remote(hr, hr, hd_s.at[0], hd_r.at[0, 0], {"head": peers[0]}).wait_send()
+        if ways:
+            tail = hr.at[:, :, rows_of(final)]
+            early = pl.ds(0, GROUPS[final][0] * rows_q)
+            whole, rest = h1.at[:, :, early], hr.at[pl.ds(0, ways - 1), :, early]
+            remote(tail, tail, hd_s.at[0], h1_r.at[0, 0], {"head": fellow}).wait_send()
+            remote(whole, whole, hd_s.at[1], h1_r.at[0, 0], {"head": fellow}).wait_send()
+            if ways > 1:
+                remote(rest, rest, hd_s.at[2], h1_r.at[0, 0], {"head": fellow}).wait_send()
         if split:
             apart = jnp.logical_not(beside)
             sent(x0_s.at[0], CHUNKS, (inner & apart) | mine[0])
@@ -705,8 +843,10 @@
             pltpu.VMEM(slab, F32),
             pltpu.VMEM(slab, F32),
             pltpu.VMEM((others, 2, nstate, rows), F32),
+            pltpu.VMEM((max(heads // 2, 1), 2, nstate, rows), F32),
+            pltpu.VMEM((max(heads // 2, 1), 2, nstate, rows), F32),
             dma((4,)),
-            dma((2,)),
+            dma((feats // WIDTH,)),
             dma((1,)),
             dma((1,)),
             dma((CHUNKS,)),
@@ -716,11 +856,12 @@
             dma((ups,)),
             dma((ups,)),
             dma((ups,)),
-            dma((ups, CHUNKS)),
+            dma((max(ups - 1, 1), CHUNKS if ups > 1 else 1)),
             dma((1,)),
             dma((len(GROUPS),)),
-            dma((1,)),
+            dma((3,)),
             dma((2, len(GROUPS))),
+            dma((2, len(GROUPS) - 1)),
         ],
         compiler_params=pltpu.CompilerParams(
             collective_id=0,

time: 40.3 us -> 37.4 us (0.928)
  Pallas kernels: 39.3 us -> 36.4 us
    pallas_call x1, Pallas kernels: 37.2 us -> 34.3 us  [local(): pl.pallas_call(functools.partial(kernel, count, heads), out_shape=(pltpu....]
where the time goes in v2:
time: 37.4 us; the launch traced here: 37.2 us
  Pallas kernels  36.4 us (97%)
  between operations  0.8 us (2%)
    pallas_call x1, Pallas kernels, local(): pl.pallas_call(functools.partial(kernel, count, heads), out_shape=(pltpu....  34.3 us
    pallas_call x1, Pallas kernels, local(): pl.pallas_call(write_out, out_shape=tuple((jax.ShapeDtypeStruct(r.shape,...  2.11 us

profile of v2, /device:TPU:0, one launch (start us, length us, event | category | flops | bytes accessed | tf_op | source)
XLA Modules:
  0.0 37.2 jit_solution(7117077916277312497)
XLA Ops:
  0.6 34.3 %shard_map.93 = (bf16[1024,1024]{1,0:T(8,128)(2,1)S(1)}, bf16[1024,1024]{1,0:T(8,128)(2,1)S(1)}, f32[256,128]{1,0:T(8,128)S(1)}, f32[256,128]{1,0:T(8,128)S(1)}) custom-call(bf16[1024,1024]{1,0:T(8,128)(2,1)} %x_hbm.1, bf16[1024,128]{1,0:T(8,128)(2,1)} %b_hbm.1, bf16[1024,128]{1,0:T(8,128)(2,1)} %c_hbm.1, bf16[1024,1024]{1,0:T(8,128)(2,1)} %d_hbm.1, ...), custom_call_target="tpu_custom_call" | custom-call | tf_op jit(solution)/shard_map/pallas_call | solution.py:805
  35.0 2.1 %shard_map.94 = (bf16[1024,1024]{1,0:T(8,128)(2,1)}, bf16[1024,1024]{1,0:T(8,128)(2,1)}, f32[256,128]{1,0:T(8,128)}, f32[256,128]{1,0:T(8,128)}) custom-call(bf16[1024,1024]{1,0:T(8,128)(2,1)S(1)} %get-tuple-element.8.refs_0_, bf16[1024,1024]{1,0:T(8,128)(2,1)S(1)} %get-tuple-element.9.refs_1_, f32[256,128]{1,0:T(8,128)S(1)} %get-tuple-element.10.refs_2_, ...), custom_call_target="tpu_custom_call" | custom-call | tf_op jit(solution)/shard_map/pallas_call | solution.py:872

commit v3 on v2

--- a/solution.py
+++ b/solution.py
@@ -14,17 +14,22 @@
 TILE = 256
 WIDTH = 256
 CHUNKS = 16
-GROUPS = ((0, 8), (8, 14), (14, 16))
-FIRST_AT = ((13.5, 16.6, 18.4), (22.6, 26.5, 28.0), (16.9, 19.9), (25.2, 27.6), (19.3, 20.7))
-INNER_AT = ((18.9, 22.3, 23.5), (24.0, 26.5, 28.0), (21.9, 25.2), (26.3, 27.6), (24.4, 25.5))
-LAST_AT = ((24.0, 27.2, 28.8), (23.0, 25.8, 27.9), (25.9, 28.7), (25.5, 28.4), (29.6, 30.2))
+GROUPS = ((0, 10), (10, 14), (14, 16))
+FIRST_AT = ((13.3, 16.6, 18.4), (22.9, 25.6, 27.0), (16.9, 19.9), (24.9, 27.1), (19.3, 20.7))
+INNER_AT = ((20.2, 22.3, 23.5), (24.0, 26.5, 28.0), (23.0, 25.2), (26.3, 28.1), (24.4, 25.5))
+LAST_AT = ((23.2, 26.2, 27.2), (21.9, 22.9, 24.9), (25.6, 28.2), (24.6, 25.8), (28.0, 28.6))
 EARLY = 2
 BEAT = 0.7
-UP_SPLIT = range(4, 16)
-DOWN_SPLIT = range(1, 11)
-TOP_SPLIT = range(12, 16)
+WAIT_FIRST = 4.0
+CROSS_LATE = 0.0
+UP_SPLIT = range(7, 15)
+TOP_UP_SPLIT = (2, 3, 4, 5)
+FIRST_SPLIT = ()
+DOWN_SPLIT = range(1, 8)
+TOP_SPLIT = range(8, 16)
 VMEM_BYTES = 67043328
 SPARE = 16384
+EXTRA = 1024 * 1024
 
 
 def scope(name):
@@ -61,8 +66,8 @@
     index_hbm,
     y_ref,
     dx_ref,
-    db_ref,
-    dc_ref,
+    sums,
+    hr,
     x_ref,
     d_ref,
     b_ref,
@@ -92,9 +97,7 @@
     tot,
     xb,
     rxb,
-    hr,
     h1,
-    sums,
     small_sem,
     x_sem,
     d_sem,
@@ -140,7 +143,10 @@
     partner = me + 1 - 2 * par
 
     def splits_up(k, q):
-        return split and k < top and q in UP_SPLIT
+        return split and q in (UP_SPLIT if k < top else TOP_UP_SPLIT)
+
+    def splits_first(q):
+        return split and q in FIRST_SPLIT
 
     def splits_down(k, q):
         return split and q in (DOWN_SPLIT if k < top else TOP_SPLIT)
@@ -151,7 +157,7 @@
     def shared(splits, k, line):
         return sum(splits(k, q) and q % 2 == line for q in range(CHUNKS))
 
-    first = col == 0
+    first, second = col == 0, col == 1
     classes = (first & inner, inner & jnp.logical_not(first), last)
 
     def carried_up(k, q):
@@ -178,17 +184,15 @@
             )
         )
     ]
-    halves = 4
-    wide = feats // halves
 
     def fill_x(n):
-        cols = pl.ds(n * wide, wide)
-        return pltpu.make_async_copy(x_hbm.at[:, cols], x_ref.at[:, cols], x_sem.at[n])
+        cols = pl.ds(n * WIDTH, WIDTH)
+        return pltpu.make_async_copy(x_hbm.at[:, cols], x_ref.at[:, cols], x_sem.at[0])
 
     fill_d = pltpu.make_async_copy(d_hbm, d_ref, d_sem.at[0])
     def load_states():
         loads[3].start()
-        for n in range(halves):
+        for n in range(strips):
             fill_x(n).start()
 
     def load_weights():
@@ -277,12 +281,11 @@
             b_t = b_ref[...].astype(F32).T.astype(BF16)
             bt_ref[...] = b_t
         with scope("xw"):
-            for n in range(halves):
-                fill_x(n).wait()
+            pltpu.make_async_copy(x_hbm, x_ref, x_sem.at[0]).wait()
         with scope("s"):
-            for n in range(halves):
-                cols = slice(n * wide, (n + 1) * wide)
-                s_buf[:, :, cols] = mm(b_t, x_ref[:, cols]).reshape(CHUNKS, rows_q, wide)
+            for q in range(strips):
+                cols = slice(q * WIDTH, (q + 1) * WIDTH)
+                s_buf[:, :, cols] = mm(b_t, x_ref[:, cols]).reshape(CHUNKS, rows_q, WIDTH)
 
     def weights():
         wide_table[...] = jnp.zeros_like(wide_table)
@@ -317,10 +320,12 @@
         with scope("barrier"):
             meet()
         for q in range(CHUNKS):
+            spared = []
             if splits_up(1, q) and q % 2:
-                pl.when(jnp.logical_not(beside & mine[1]))(x0_copy(q).start)
-            else:
-                x0_copy(q).start()
+                spared.append(beside & mine[1])
+            if splits_first(q):
+                spared.append(first & mine[1])
+            when(jnp.logical_not(functools.reduce(jnp.logical_or, spared)) if spared else None, x0_copy(q).start)
         with scope("tw"):
             for load in loads[:3]:
                 load.wait()
@@ -404,7 +409,7 @@
             weight = jnp.where(differ >= 1 << n, w_rows[:, n + 1 : n + 2], weight)
         return jnp.where(at <= row, weight, 0.0)
 
-    def weigh(i):
+    def weigh_diagonal(i):
         rows = slice(i * TILE, (i + 1) * TILE)
         w_rows = w_ref[rows, :]
         upper, lower = w_rows[:half], w_rows[half:]
@@ -416,35 +421,46 @@
             ],
             axis=0,
         )
+        mix[rows, rows] = (mm_nt(c_ref[rows, :], b_ref[rows, :]) * weight).astype(BF16)
+        d_mix[rows, rows] = (mm_nt(d_ref[rows, :], x_ref[rows, :]) * weight).astype(BF16)
+
+    def weigh(i):
+        rows = slice(i * TILE, (i + 1) * TILE)
+        w_rows = w_ref[rows, :]
         c_i, d_i = c_ref[rows, :], d_ref[rows, :]
-        for j in range(i + 1):
+        for j in range(i):
             cols = slice(j * TILE, (j + 1) * TILE)
-            if j < i:
-                level = tile_bits + (i ^ j).bit_length()
-                factor = w_rows[:, level : level + 1]
-            else:
-                factor = weight
+            level = tile_bits + (i ^ j).bit_length()
+            factor = w_rows[:, level : level + 1]
             mix[rows, cols] = (mm_nt(c_i, b_ref[cols, :]) * factor).astype(BF16)
             d_mix[rows, cols] = (mm_nt(d_i, x_ref[cols, :]) * factor).astype(BF16)
 
-    def near_y(i):
+    def near_y(i, n0, n1):
         rows = slice(i * TILE, (i + 1) * TILE)
         seen = slice(0, (i + 1) * TILE)
-        y_acc[rows, :] = mm(mix[rows, seen], x_ref[seen, :])
-        grads[1, :, rows] = mm_nt(bt_ref[:, seen], d_mix[rows, seen])
-
-    def near_dx(j):
+        part_y = slice(n0 * feats // 2, n1 * feats // 2)
+        y_acc[rows, part_y] = mm(mix[rows, seen], x_ref[seen, part_y])
+        if n0 == 0:
+            grads[1, :, rows] = mm_nt(bt_ref[:, seen], d_mix[rows, seen])
+
+    def near_dx(j, n0, n1):
         cols = slice(j * TILE, (j + 1) * TILE)
         seen = slice(j * TILE, toks)
-        dx_acc[cols, :] = mm_tn(mix[seen, cols], d_ref[seen, :])
-        grads[0, :, cols] = mm(ct_ref[:, seen], d_mix[seen, cols])
-
-    def source(k, q):
+        part_x = slice(n0 * feats // 2, n1 * feats // 2)
+        dx_acc[cols, part_x] = mm_tn(mix[seen, cols], d_ref[seen, part_x])
+        if n0 == 0:
+            grads[0, :, cols] = mm(ct_ref[:, seen], d_mix[seen, cols])
+
+    def source(k, q, line=None):
         here = low_top[k]
         if k == 1 and splits_up(1, q):
             here = here & jnp.logical_not(beside & mine[1 - q % 2])
             if q % 2 == 0:
                 pl.when(beside & mine[1])(x0_copy(q).wait_recv)
+        if k == 1 and splits_first(q):
+            here = here & jnp.logical_not(first & mine[0])
+        if line is not None:
+            here = here & mine[line]
 
         @pl.when(here)
         def _():
@@ -452,12 +468,14 @@
             group = s_buf[q] + rx0[q]
             for j in range(1, k):
                 up_copy(j, q).wait_recv()
+                if j == 1 and line == 1:
+                    pl.when(second)(gather_copy(1, q).start)
                 group = group + rc[j - 1, q]
             up[q] = group
             up_copy(k, q).start()
 
-    def relay_up(k, q):
-        @pl.when(relay[k])
+    def relay_up(k, q, line=None):
+        @pl.when(relay[k] if line is None else relay[k] & mine[line])
         def _():
             up_copy(k, q).wait_recv()
             when(carried_up(k, q), forward_copy(k, q).start)
@@ -510,8 +528,17 @@
             for j in range(1, k):
                 g_buf[j, q] = g_buf[j, q] + got
                 back_copy(j, q).start()
-            cross(q)
-            xb_copy(q).start()
+            if k == 2 and split:
+                pl.when(jnp.logical_not(second))(lambda: send_cross(q))
+            else:
+                send_cross(q)
+
+    def send_cross(q):
+        cross(q)
+        xb_copy(q).start()
+
+    def cross_late(q):
+        pl.when(second)(lambda: send_cross(q))
 
     def beside_down(q):
         def own():
@@ -544,6 +571,7 @@
     def spread(array, g):
         rows = rows_of(g)
         if g == final:
+            sums[0, array, rows] = grads[array, rows, lanes_of(head)]
             for m, peer in enumerate(peers):
                 remote(
                     grads.at[array, rows, lanes_of(peer)],
@@ -673,19 +701,26 @@
 
     for q in range(CHUNKS):
         for k in levels:
-            put(rise_at(k, q), "source", source, k, q)
+            apart = 2 if k == 2 and splits_first(q) else 0
+            for line in range(apart):
+                put(rise_at(k, q) + WAIT_FIRST * (1 - line), "source", source, k, q, line)
+                put(rise_at(k, q) + 3.4 + WAIT_FIRST * (1 - line), "relay_up", relay_up, k, q, line)
+            if not apart:
+                put(rise_at(k, q), "source", source, k, q)
             put(fall_at(k, q), "pass_down", pass_down, k, q)
             if k > 1:
-                put(rise_at(k, q) + 3.4, "relay_up", relay_up, k, q)
+                if not apart:
+                    put(rise_at(k, q) + 3.4, "relay_up", relay_up, k, q)
                 put(6.4 + lead(q) if k == top else fall_at(k, q) - 1.4, "relay_down", relay_down, k, q)
             if splits_up(k, q):
-                put(rise_at(k, q) + 3.6 + 0.1 * q, "gather", gather, k, q)
+                put(rise_at(k, q) + (3.6 + 0.1 * q if k < top else 6.6), "gather", gather, k, q)
             if k < top:
-                put(8.4 + 0.28 * q, "descend", descend, k, q)
+                put(8.8 + 0.35 * q, "descend", descend, k, q)
             elif splits_down(k, q):
-                put(6.9 + 0.2 * (q - TOP_SPLIT[0]), "descend", descend, k, q)
+                put(6.2 + 0.3 * (q - TOP_SPLIT[0]), "descend", descend, k, q)
         if split:
-            put(16.0 + 0.45 * q, "beside", beside_down, q)
+            put(fall_at(2, q) + CROSS_LATE, "cross", cross_late, q)
+            put(15.0 + 0.45 * q + 0.23 * max(q - 7, 0), "beside", beside_down, q)
         if q >= EARLY:
             put(8.0 + 0.95 * (q - EARLY), "late", late_sends, q)
     deeper = max(top - 2, 0)
@@ -697,19 +732,24 @@
             put(downs[g] + later, "far_down", far_down, g, which)
             if g != final:
                 put(up_halves[g] + later, "halfway", halfway, 1, g, which)
-                if g == final - 1:
+                if g + 1 < final:
                     put(down_halves[g] + later, "halfway", halfway, 0, g, which, 0)
-                    put(max(down_halves[g], downs[final]) + 0.1 + later, "halfway", halfway, 0, g, which, 1)
+                    put(max(down_halves[g], downs[g + 1]) + 0.1 + later, "halfway", halfway, 0, g, which, 1)
                 else:
                     put(down_halves[g] + later, "halfway", halfway, 0, g, which)
         for n in range(2):
             put(ys[n] + later, "finish_y", finish_y, n, which)
-    near = [(weigh, 0)]
+    def pieces(step, i, long):
+        return [(step, i, 0, 1), (step, i, 1, 2)] if long else [(step, i, 0, 2)]
+
+    near = [(weigh_diagonal, 0)]
     for i in range(1, blocks):
-        near += [(weigh, i), (near_y, i - 1)]
-    near += [(near_y, blocks - 1)] + [(near_dx, j) for j in range(blocks)]
-    for n, (step, i) in enumerate(near):
-        put(4.3 + 13.2 / len(near) * n, step.__name__, step, i)
+        near += [(weigh_diagonal, i), (weigh, i)] + pieces(near_y, i - 1, i > blocks // 2)
+    near += pieces(near_y, blocks - 1, True)
+    for j in range(blocks):
+        near += pieces(near_dx, j, j < blocks // 2)
+    for n, (step, *args) in enumerate(near):
+        put(4.1 + 13.0 / len(near) * n, step.__name__, step, *args)
     put(18.6, "rises", rises)
     for _, _, name, step, args in sorted(plan, key=lambda item: item[:2]):
         with scope(name + "_" + "_".join(str(a) for a in args)):
@@ -719,29 +759,13 @@
         for q in range(strips):
             cols = slice(q * WIDTH, (q + 1) * WIDTH)
             dx_ref[:, cols] = (dx_acc[:, cols] + mm(b_ref[...], back[:, cols])).astype(BF16)
-    def finish(array):
-        parts = []
-        for g in range(len(GROUPS)):
-            rows = rows_of(g)
-            if g == final:
-                ahead, total = heads - 1, grads[array, rows, lanes_of(head)]
-            else:
-                ahead, total = max(ways - 1, 0), sums[0, array, rows]
-            if ahead:
-                given = hr.at[pl.ds(0, ahead), array, rows]
-                remote(given, given, hd_s.at[0], hd_r.at[array, g], {"head": fellow}).wait_recv()
-            for m in range(ahead):
-                total = total + hr[m, array, rows]
-            parts.append(total)
-        (db_ref, dc_ref)[array][...] = jnp.concatenate(parts, axis=0).T
-
-    for ending in range(2):
-
-        @pl.when(last if ending else inner)
-        def _():
-            for array in (0, 1) if ending else (1, 0):
-                with scope(f"heads_{array}_{ending}"):
-                    finish(array)
+    with scope("heads"):
+        for array in range(2):
+            for g in range(len(GROUPS)):
+                ahead = heads - 1 if g == final else max(ways - 1, 0)
+                if ahead:
+                    given = hr.at[pl.ds(0, ahead), array, rows_of(g)]
+                    remote(given, given, hd_s.at[0], hd_r.at[array, g], {"head": fellow}).wait_recv()
 
     def sent(sem, n, condition):
         if n:
@@ -759,7 +783,11 @@
                 remote(rest, rest, hd_s.at[2], h1_r.at[0, 0], {"head": fellow}).wait_send()
         if split:
             apart = jnp.logical_not(beside)
-            sent(x0_s.at[0], CHUNKS, (inner & apart) | mine[0])
+            lesser = sum(splits_first(q) for q in range(CHUNKS))
+            sent(x0_s.at[0], CHUNKS, mine[0] | (inner & apart & jnp.logical_not(first)))
+            sent(x0_s.at[0], CHUNKS - lesser, first & mine[1])
+            sent(up_s.at[0], CHUNKS - lesser, first & mine[0])
+            sent(ga_s.at[0], lesser, second & mine[1])
             sent(x0_s.at[0], owned(splits_up, 1, 0), beside & mine[1])
             sent(xb_s.at[0], CHUNKS, (inner & apart) | mine[1])
             sent(xb_s.at[0], owned(splits_down, 1, 0), beside & mine[0])
@@ -770,7 +798,8 @@
             for line in range(2):
                 full = mine[line] & jnp.logical_not(beside)
                 edge = mine[line] & beside
-                sent(up_s.at[0], CHUNKS, low_top[k] & full)
+                most = full & jnp.logical_not(first) if split and k == 1 and line == 0 else full
+                sent(up_s.at[0], CHUNKS, low_top[k] & most)
                 sent(up_s.at[0], owned(splits_up, k, line), low_top[k] & edge)
                 sent(fw_s.at[k - 1], CHUNKS, relay[k] & full)
                 sent(fw_s.at[k - 1], owned(splits_up, k, line), relay[k] & edge)
@@ -780,9 +809,24 @@
                 sent(bk_s.at[k - 1], owned(splits_down, k, line), last & mine[line])
 
 
-def write_out(*refs):
-    copies = [pltpu.make_async_copy(refs[n], refs[n + 4], refs[8].at[n]) for n in range(4)]
-    for copy in copies:
+def write_out(heads, y_ref, dx_ref, sums, hr, y_hbm, dx_hbm, db_hbm, dc_hbm, db_ref, dc_ref, sem):
+    copies = [
+        pltpu.make_async_copy(src, dst, sem.at[n])
+        for n, (src, dst) in enumerate(
+            ((y_ref, y_hbm), (dx_ref, dx_hbm), (dc_ref, dc_hbm), (db_ref, db_hbm))
+        )
+    ]
+    copies[0].start()
+    copies[1].start()
+    nstate = sums.shape[2]
+    edge = GROUPS[-1][0] * (nstate // CHUNKS)
+    for array, ref, copy in ((1, dc_ref, copies[2]), (0, db_ref, copies[3])):
+        early, tail = sums[0, array, :edge], sums[0, array, edge:]
+        for m in range(heads // 2 - 1):
+            early = early + hr[m, array, :edge]
+        for m in range(heads - 1):
+            tail = tail + hr[m, array, edge:]
+        ref[...] = jnp.concatenate([early, tail], axis=0).T
         copy.start()
     for copy in copies:
         copy.wait()
@@ -807,8 +851,8 @@
         out_shape=(
             pltpu.VMEM((toks, feats), BF16),
             pltpu.VMEM((toks, feats), BF16),
-            pltpu.VMEM((rows, nstate), F32),
-            pltpu.VMEM((rows, nstate), F32),
+            pltpu.VMEM((max(heads // 2, 1), 2, nstate, rows), F32),
+            pltpu.VMEM((others, 2, nstate, rows), F32),
         ),
         in_specs=[hbm] * 6,
         out_specs=(vmem,) * 4,
@@ -842,11 +886,9 @@
             pltpu.VMEM(slab, F32),
             pltpu.VMEM(slab, F32),
             pltpu.VMEM(slab, F32),
-            pltpu.VMEM((others, 2, nstate, rows), F32),
-            pltpu.VMEM((max(heads // 2, 1), 2, nstate, rows), F32),
             pltpu.VMEM((max(heads // 2, 1), 2, nstate, rows), F32),
             dma((4,)),
-            dma((feats // WIDTH,)),
+            dma((1,)),
             dma((1,)),
             dma((1,)),
             dma((CHUNKS,)),
@@ -866,16 +908,22 @@
         compiler_params=pltpu.CompilerParams(
             collective_id=0,
             has_side_effects=True,
-            vmem_limit_bytes=VMEM_BYTES - 4 * toks * feats - 8 * rows * nstate - SPARE,
+            vmem_limit_bytes=VMEM_BYTES - 4 * toks * feats - 8 * (max(heads // 2, 1) + others) * rows * nstate - SPARE - EXTRA,
         ),
     )(x_in, b_in, c_in, d_out, table, index)
+    slices = jax.ShapeDtypeStruct((rows, nstate), F32)
+    wholes = jax.ShapeDtypeStruct((toks, feats), BF16)
     return pl.pallas_call(
-        write_out,
-        out_shape=tuple(jax.ShapeDtypeStruct(r.shape, r.dtype) for r in results),
+        functools.partial(write_out, heads),
+        out_shape=(wholes, wholes, slices, slices),
         in_specs=[vmem] * 4,
         out_specs=(hbm,) * 4,
-        scratch_shapes=[dma((4,))],
-        compiler_params=pltpu.CompilerParams(vmem_limit_bytes=1024 * 1024),
+        scratch_shapes=[
+            pltpu.VMEM((rows, nstate), F32),
+            pltpu.VMEM((rows, nstate), F32),
+            dma((4,)),
+        ],
+        compiler_params=pltpu.CompilerParams(vmem_limit_bytes=2 * 1024 * 1024),
     )(*results)
 
 

time: 37.4 us -> 37.3 us (level)
  no operation moved by 1% of the time
where the time goes in v3:
time: 37.3 us; the launch traced here: 37.2 us
  Pallas kernels  36.4 us (98%)
  between operations  0.8 us (2%)
    pallas_call x1, Pallas kernels, local(): pl.pallas_call(functools.partial(kernel, count, heads), out_shape=(pltpu....  34.3 us
    pallas_call x1, Pallas kernels, local(): pl.pallas_call(functools.partial(write_out, heads), out_shape=(wholes, wh...  2.11 us

profile of v3, /device:TPU:0, one launch (start us, length us, event | category | flops | bytes accessed | tf_op | source)
XLA Modules:
  0.0 37.2 jit_solution(138214006038885602)
XLA Ops:
  0.6 34.3 %shard_map.93 = (bf16[1024,1024]{1,0:T(8,128)(2,1)S(1)}, bf16[1024,1024]{1,0:T(8,128)(2,1)S(1)}, f32[2,2,128,256]{3,2,1,0:T(8,128)S(1)}, f32[3,2,128,256]{3,2,1,0:T(8,128)S(1)}) custom-call(bf16[1024,1024]{1,0:T(8,128)(2,1)} %x_hbm.1, bf16[1024,128]{1,0:T(8,128)(2,1)} %b_hbm.1, bf16[1024,128]{1,0:T(8,128)(2,1)} %c_hbm.1, bf16[1024,1024]{1,0:T(8,128)(2,1)} %d_hbm.1, ...), custom_call_target="tpu_custom_call" | custom-call | tf_op jit(solution)/shard_map/pallas_call | solution.py:849
  34.9 2.1 %shard_map.94 = (bf16[1024,1024]{1,0:T(8,128)(2,1)}, bf16[1024,1024]{1,0:T(8,128)(2,1)}, f32[256,128]{1,0:T(8,128)}, f32[256,128]{1,0:T(8,128)}) custom-call(bf16[1024,1024]{1,0:T(8,128)(2,1)S(1)} %get-tuple-element.8.y_ref, bf16[1024,1024]{1,0:T(8,128)(2,1)S(1)} %get-tuple-element.9.dx_ref, f32[2,2,128,256]{3,2,1,0:T(8,128)S(1)} %get-tuple-element.10.sums, ...), custom_call_target="tpu_custom_call" | custom-call | tf_op jit(solution)/shard_map/pallas_call | solution.py:916
